TPU v7x, 512 devices: a whole 4x4x16 slice. The times are simulated.
512 devices in a mesh: guide: 2 (over core), dp: 16 (over y, x), mp: 16 (over z).
Axes of the slice: x: 4, y: 4, z: 16, core: 2. Of those that a mesh axis runs over, the one named last changes fastest.
Arguments:
- states: bfloat16 [2, 128, 2048], P('guide', 'dp'), may hold values from -6 to 6
- lengths: int32 [2, 128], P('guide', 'dp'), may hold values from 1 to 32768, as said below
- sink_cache: bfloat16 [2, 128, 16, 2, 4, 128], P('guide', 'dp', 'mp'), may hold values from -48 to 48
- window_cache: bfloat16 [2, 128, 16, 2, 256, 128], P('guide', 'dp', 'mp'), may hold values from -360 to 360
- qkv_weight: bfloat16 [2048, 3, 16, 128], P(None, None, 'mp'), may hold values from -0.125 to 0.125
- out_weight: bfloat16 [16, 128, 2048], P('mp'), may hold values from -0.125 to 0.125
- expert_ids: int32 [2, 128, 8], replicated, may hold values from 0 to 63, all different within a row; in each aligned block of 8 rows (0 to 7, 8 to 15, ..., all dimensions but the last counted through in order) at most 2 rows name the same one
- route_weight: float32 [2, 128, 8], replicated, may hold values from 0.5 to 2
- expert_in: bfloat16 [2, 2048, 65536], P(None, None, ('guide', 'dp', 'mp')), may hold values from -0.125 to 0.125
- expert_out: bfloat16 [65536, 2048], P(('guide', 'dp', 'mp')), may hold values from -0.1875 to 0.1875
- vocab_weight: bfloat16 [2048, 26624], P(('guide', 'dp'), 'mp'), may hold values from -0.125 to 0.125
- guidance: float32 [128], P('dp'), may hold values from 1 to 5
Outputs:
- guided: float32 [128, 16, 2, 832], P('dp', 'mp', 'guide')
Inputs may be any that keep to these rules, and one draw needn't show every extreme that they name: `lengths`: one stream of one request has exactly 32768 cached positions. `expert_ids`: taking the tokens streams first, then requests, in aligned blocks of 8 tokens (the tokens of one device), no expert is named by more than 2 tokens of a block, a bound that some block reaches.
All inputs are finite; a program needn't handle non-finite values.
Results may differ from a plain program's by a relative error of at most 0.025.
Values may be sent and summed in bfloat16 or wider, within the bound.
A program may use at most 64 MiB of HBM per device.

v0:
```python
import math

import jax
import jax.numpy as jnp
from jax import lax
from jax.sharding import PartitionSpec as P

FFE = 1024


EPSILON = 1e-05


def partner(block, axis, stride):
    count = lax.axis_size(axis)
    route = []
    for low in range(count):
        high = low | 1 << stride
        if high != low and high < count:
            route += [(low, high), (high, low)]
    return lax.ppermute(block, axis, route)


def rms_norm(values):
    return values * lax.rsqrt(jnp.mean(values * values, axis=-1, keepdims=True) + EPSILON)


def rotate(vectors, positions):
    full_width = vectors.shape[-1]
    half_width = full_width // 2
    step_index = jnp.arange(half_width, dtype=jnp.float32)
    inverse = jnp.exp(step_index * (-2.0 * math.log(10000.0) / full_width))
    angles = positions.astype(jnp.float32)[:, None] * inverse[None, :]
    cosine = jnp.cos(angles)[:, None, :]
    sine_part = jnp.sin(angles)[:, None, :]
    first_half = vectors[..., :half_width]
    second = vectors[..., half_width:]
    return jnp.concatenate(
        [first_half * cosine - second * sine_part, second * cosine + first_half * sine_part],
        axis=-1,
    )


def body(
    states,
    lengths,
    sink_cache,
    window_cache,
    qkv_weight,
    out_weight,
    expert_ids,
    route_weight,
    expert_in,
    expert_out,
    vocab_weight,
    guidance,
):
    hidden = states[0]
    own_lengths = lengths[0]
    request_count = hidden.shape[0]
    normed = rms_norm(hidden.astype(jnp.float32)).astype(jnp.bfloat16)
    projected = jnp.einsum("rd,dthe->rthe", normed, qkv_weight, preferred_element_type=jnp.float32)
    query_rot = rotate(projected[:, 0], own_lengths).astype(jnp.bfloat16)
    fresh_key = rotate(projected[:, 1], own_lengths).astype(jnp.bfloat16)
    fresh_value = projected[:, 2].astype(jnp.bfloat16)
    sink_rows = sink_cache[0]
    window_rows = window_cache[0]
    sink_count = sink_rows.shape[3]
    window_count = window_rows.shape[3]
    root_size = math.sqrt(query_rot.shape[-1])
    sink_scores = (
        jnp.einsum(
            "rhe,rhse->rhs", query_rot, sink_rows[:, :, 0], preferred_element_type=jnp.float32
        )
        / root_size
    )
    window_scores = (
        jnp.einsum(
            "rhe,rhwe->rhw", query_rot, window_rows[:, :, 0], preferred_element_type=jnp.float32
        )
        / root_size
    )
    self_scores = (
        jnp.einsum("rhe,rhe->rh", query_rot, fresh_key, preferred_element_type=jnp.float32)
        / root_size
    )
    length_limit = own_lengths[:, None, None]
    sink_valid = jnp.arange(sink_count, dtype=jnp.int32)[None, None, :] < length_limit
    window_valid = (
        jnp.arange(window_count, dtype=jnp.int32)[None, None, :]
        >= sink_count + window_count - length_limit
    )
    sink_scores = jnp.where(sink_valid, sink_scores, -1e30)
    window_scores = jnp.where(window_valid, window_scores, -1e30)
    highest = jnp.maximum(
        jnp.maximum(jnp.max(sink_scores, axis=-1), jnp.max(window_scores, axis=-1)), self_scores
    )
    sink_exp = jnp.exp(sink_scores - highest[..., None])
    window_exp = jnp.exp(window_scores - highest[..., None])
    self_exp = jnp.exp(self_scores - highest)
    totals = jnp.sum(sink_exp, axis=-1) + jnp.sum(window_exp, axis=-1) + self_exp
    sink_prob = (sink_exp / totals[..., None]).astype(jnp.bfloat16)
    window_prob = (window_exp / totals[..., None]).astype(jnp.bfloat16)
    self_prob = (self_exp / totals).astype(jnp.bfloat16)
    mixture = (
        jnp.einsum(
            "rhs,rhse->rhe", sink_prob, sink_rows[:, :, 1], preferred_element_type=jnp.float32
        )
        + jnp.einsum(
            "rhw,rhwe->rhe", window_prob, window_rows[:, :, 1], preferred_element_type=jnp.float32
        )
        + self_prob[..., None].astype(jnp.float32) * fresh_value.astype(jnp.float32)
    ).astype(jnp.bfloat16)
    partial_out = jnp.einsum("rhe,hed->rd", mixture, out_weight, preferred_element_type=jnp.float32)
    attention_out = lax.psum(partial_out, "mp")
    residual = (hidden.astype(jnp.float32) + attention_out).astype(jnp.bfloat16)
    moe_in = rms_norm(residual.astype(jnp.float32)).astype(jnp.bfloat16)
    unit_count = expert_in.shape[2]
    unit_start = lax.axis_index(("guide", "dp", "mp")) * unit_count
    unit_expert = (unit_start + jnp.arange(unit_count, dtype=jnp.int32)) // FFE
    choice_rows = expert_ids.reshape(-1, expert_ids.shape[-1])
    route_rows = route_weight.reshape(-1, route_weight.shape[-1])
    coefficient = jnp.sum(
        jnp.where(
            choice_rows[:, :, None] == unit_expert[None, None, :], route_rows[:, :, None], 0.0
        ),
        axis=1,
    )
    piece = lax.all_gather(moe_in, ("guide", "dp"), axis=0, tiled=True)
    gate = jnp.dot(piece, expert_in[0], preferred_element_type=jnp.float32)
    upward = jnp.dot(piece, expert_in[1], preferred_element_type=jnp.float32)
    activated = (jax.nn.silu(gate) * upward * coefficient).astype(jnp.bfloat16)
    expert_terms = jnp.dot(activated, expert_out, preferred_element_type=jnp.float32)
    expert_part = lax.psum_scatter(expert_terms, ("guide", "dp"), scatter_dimension=0, tiled=True)
    expert_total = lax.psum(expert_part, "mp")
    final = rms_norm(residual.astype(jnp.float32) + expert_total).astype(jnp.bfloat16)
    final_all = lax.all_gather(final, ("guide", "dp"), axis=0, tiled=True)
    row_share = vocab_weight.shape[0]
    share_start = lax.axis_index(("guide", "dp")) * row_share
    final_cols = lax.dynamic_slice_in_dim(final_all, share_start, row_share, 1)
    logits = lax.psum_scatter(
        jnp.dot(final_cols, vocab_weight, preferred_element_type=jnp.float32).astype(jnp.bfloat16),
        ("guide", "dp"),
        scatter_dimension=0,
        tiled=True,
    ).astype(jnp.float32)
    half_width = logits.shape[1] // 2
    stream_index = lax.axis_index("guide")
    own_half = lax.dynamic_slice_in_dim(logits, stream_index * half_width, half_width, 1)
    other_half = lax.dynamic_slice_in_dim(logits, (1 - stream_index) * half_width, half_width, 1)
    partner_logits = partner(other_half, "guide", 0)
    is_conditional = stream_index == 0
    conditional = jnp.where(is_conditional, own_half, partner_logits)
    unconditional = jnp.where(is_conditional, partner_logits, own_half)
    guided = unconditional + guidance[:, None] * (conditional - unconditional)
    return guided.reshape(request_count, 1, 1, half_width)


def solution(mesh):
    in_specs = (
        P("guide", "dp", None),
        P("guide", "dp"),
        P("guide", "dp", "mp", None, None, None),
        P("guide", "dp", "mp", None, None, None),
        P(None, None, "mp", None),
        P("mp", None, None),
        P(),
        P(),
        P(None, None, ("guide", "dp", "mp")),
        P(("guide", "dp", "mp"), None),
        P(("guide", "dp"), "mp"),
        P("dp"),
    )
    out_specs = P("dp", "mp", "guide", None)
    return jax.shard_map(body, mesh=mesh, in_specs=in_specs, out_specs=out_specs, check_vma=False)
```

profile of v0, /device:TPU:1, one launch (start us, length us, event | category | flops | bytes accessed | tf_op | source)
XLA Modules:
  0.0 657.1 jit_solution(2036525778644055514)
XLA Ops:
  6.6 0.8 bitcast_convert_fusion
  7.4 0.8 broadcast_subtract_fusion
  8.2 0.9 fusion.23
  9.1 1.2 fusion
  12.1 0.9 fusion.11
  13.0 128.0 %all-reduce.5.cloned.1.call-done = f32[8,2048]{1,0:T(8,128)} async-done(((f32[8,2048]{1,0:T(8,128)}), f32[8,2048]{1,0:T(8,128)}) %all-reduce.5.cloned.1.call-update) | async-done | bytes 65552 | tf_op jit(solution)/shard_map/psum | solution.py:115
  141.0 1.0 fusion.26
  142.0 0.7 fusion.27
  143.1 1.3 select_reduce_fusion
  144.4 65.6 %all-gather.3.cloned.1.call-done = bf16[256,2048]{1,0:T(8,128)(2,1)} async-done(((bf16[8,2048]{1,0:T(8,128)(2,1)}), bf16[256,2048]{1,0:T(8,128)(2,1)}) %all-gather.3.cloned.1.call-update) | async-done | bytes 1048592 | tf_op jit(solution)/shard_map/all_gather | solution.py:129
  210.0 1.9 fusion.9
  211.9 3.2 fusion.4
  215.2 99.4 %reduce-scatter.2.cloned.1.call-done = f32[8,2048]{1,0:T(8,128)} async-done(((f32[256,2048]{1,0:T(8,128)}), f32[8,2048]{1,0:T(8,128)}) %reduce-scatter.2.cloned.1.call-update) | async-done | bytes 65552 | tf_op jit(solution)/shard_map/reduce_scatter | solution.py:134
  314.6 125.9 %all-reduce.7.cloned.1.call-done = f32[8,2048]{1,0:T(8,128)} async-done(((f32[8,2048]{1,0:T(8,128)}), f32[8,2048]{1,0:T(8,128)}) %all-reduce.7.cloned.1.call-update) | async-done | bytes 65552 | tf_op jit(solution)/shard_map/psum | solution.py:135
  440.5 1.0 multiply_reduce_fusion
  441.5 1.5 multiply_convert_fusion
  443.1 65.8 %all-gather.5.cloned.1.call-done = bf16[256,2048]{1,0:T(8,128)(2,1)} async-done(((bf16[8,2048]{1,0:T(8,128)(2,1)}), bf16[256,2048]{1,0:T(8,128)(2,1)}) %all-gather.5.cloned.1.call-update) | async-done | bytes 1048592 | tf_op jit(solution)/shard_map/all_gather | solution.py:137
  508.9 2.2 convolution_convert_fusion
  511.1 1.3 dynamic-slice
  513.1 132.5 %all-reduce.9.cloned.1.call-done = bf16[256,1664]{1,0:T(8,128)(2,1)} async-done(((bf16[256,1664]{1,0:T(8,128)(2,1)}), bf16[256,1664]{1,0:T(8,128)(2,1)}) %all-reduce.9.cloned.1.call-update) | async-done | bytes 851984
  645.6 0.7 dynamic-slice_convert_fusion
  646.4 2.3 collective-permute-start
  648.7 0.8 collective-permute-done
  649.6 0.6 copy.26
  (64 shorter events, 2.6 us)
Async XLA Ops:
  6.5 2.5 copy-start
  6.5 4.8 copy-start.9
  6.5 3.9 copy-start.5
  6.5 4.2 copy-start.11
  6.5 5.6 copy-start.3
  6.5 134.5 %all-reduce.5.cloned.1.call-start = ((), (), s32[]{:S(2)}) async-start(), calls=%async_computation.1 | async-start | bytes 131072 | tf_op jit(solution)/shard_map/psum | solution.py:115
  9.1 131.9 %copy-start.4 = (bf16[1,8,2048]{2,1,0:T(8,128)(2,1)S(1)}, bf16[1,8,2048]{2,1,0:T(8,128)(2,1)}, u32[]{:S(2)}) copy-start(bf16[1,8,2048]{2,1,0:T(8,128)(2,1)} %param.12) | copy-start | bytes 98308
  9.1 133.7 %copy-start.7 = (s32[2,128,8]{1,2,0:T(8,128)S(1)}, s32[2,128,8]{1,2,0:T(8,128)}, u32[]{:S(2)}) copy-start(s32[2,128,8]{1,2,0:T(8,128)} %param.18) | copy-start | bytes 24580
  10.3 132.6 %copy-start.8 = (f32[2,128,8]{1,2,0:T(8,128)S(1)}, f32[2,128,8]{1,2,0:T(8,128)}, u32[]{:S(2)}) copy-start(f32[2,128,8]{1,2,0:T(8,128)} %param.19) | copy-start | bytes 24580
  12.1 199.8 %copy-start.2 = (bf16[128,2048]{1,0:T(8,128)(2,1)S(1)}, bf16[128,2048]{1,0:T(8,128)(2,1)}, u32[]{:S(2)}) copy-start(bf16[128,2048]{1,0:T(8,128)(2,1)} %param.21) | copy-start | bytes 1572868
  13.0 197.0 %all-gather.3.cloned.1.call-start = ((), (), s32[]{:S(2)}) async-start(), calls=%async_computation.2 | async-start | bytes 1081344 | tf_op jit(solution)/shard_map/all_gather | solution.py:129
  142.7 171.9 %reduce-scatter.2.cloned.1.call-start = ((), (), s32[]{:S(2)}) async-start(), calls=%async_computation.3 | async-start | bytes 2162688 | tf_op jit(solution)/shard_map/reduce_scatter | solution.py:134
  210.0 1.9 copy-start.1
  215.1 293.8 %copy-start.6 = (bf16[64,1664]{1,0:T(8,128)(2,1)S(1)}, bf16[64,1664]{1,0:T(8,128)(2,1)}, u32[]{:S(2)}) copy-start(bf16[64,1664]{1,0:T(8,128)(2,1)} %param.22) | copy-start | bytes 638980
  215.1 434.4 %copy-start.10 = (f32[8]{0:T(128)S(1)}, f32[8]{0:T(128)}, u32[]{:S(2)}) copy-start(f32[8]{0:T(128)} %param.23) | copy-start | bytes 100
  215.1 225.4 %all-reduce.7.cloned.1.call-start = ((), (), s32[]{:S(2)}) async-start(), calls=%async_computation.4 | async-start | bytes 131072 | tf_op jit(solution)/shard_map/psum | solution.py:135
  314.6 194.3 %all-gather.5.cloned.1.call-start = ((), (), s32[]{:S(2)}) async-start(), calls=%async_computation.5 | async-start | bytes 1081344 | tf_op jit(solution)/shard_map/all_gather | solution.py:137
  443.1 202.6 %all-reduce.9.cloned.1.call-start = ((), (), s32[]{:S(2)}) async-start(), calls=%async_computation.6 | async-start | bytes 1703936
  646.4 3.1 collective-permute-start
Sparse Core Ops, SparseCore 0:
  13.1 127.8 all-reduce.4
  144.7 65.3 all-gather.2
  215.3 99.2 reduce-scatter.1
  316.9 123.6 all-reduce.6
  443.6 65.3 all-gather.4
  512.1 133.5 all-reduce.8
where the time goes:
time: 658 us; the launch traced here: 657 us
  waiting for transfers between devices  618 us (94%)
  between operations  14.4 us (2%)
  matrix products  9.92 us (2%)
  other arithmetic  9.7 us (1%)
    unnamed x7, waiting for transfers between devices  133 us
    psum x1, waiting for transfers between devices, body(): attention_out = lax.psum(partial_out, 'mp')  128 us
    psum x1, waiting for transfers between devices, body(): expert_total = lax.psum(expert_part, 'mp')  126 us
    reduce_scatter x1, waiting for transfers between devices, body(): lax.psum_scatter(expert_terms, ('guide', 'dp'), scatter_dimension=0, tile...  99.4 us
    all_gather x1, waiting for transfers between devices, body(): final_all = lax.all_gather(final, ('guide', 'dp'), axis=0, tiled=True)  65.8 us
    all_gather x1, waiting for transfers between devices, body(): piece = lax.all_gather(moe_in, ('guide', 'dp'), axis=0, tiled=True)  65.6 us
  transfers between devices with their start and end apart: 7, of which 7 were waited for; matrix products, arithmetic and copies ran while one was open for 0% of the time, Pallas kernels for 0%

commit v1 on v0

v1 whole, which is shorter than its diff:
```python
import math

import jax
import jax.numpy as jnp
from jax import lax
from jax.experimental import pallas as pl
from jax.experimental.pallas import tpu as pltpu
from jax.sharding import PartitionSpec as P

F32 = jnp.float32
BF16 = jnp.bfloat16
EPSILON = 1e-05
MESH = pl.DeviceIdType.MESH
D = 2048
HD = 128
R = 8
NZ = 16
ND = 16
NP = 32
SINKS = 4
WINDOW = 256
HALF = 832
WIDE = 896
NEG = -1e30


def iota(shape, axis):
    return lax.broadcasted_iota(jnp.int32, shape, axis)


def dot(a, b):
    return jnp.dot(a, b, preferred_element_type=F32)


def dot_nt(a, b):
    return lax.dot_general(a, b, (((1,), (1,)), ((), ())), preferred_element_type=F32)


def column(row):
    square = jnp.broadcast_to(row, (R, R))
    return jnp.sum(jnp.where(iota((R, R), 0) == iota((R, R), 1), square, 0.0), axis=1, keepdims=True)


def kernel(
    states_h, lengths_h, sink_h, window_h, qkv_h, outw_h, ids_h, route_h, ein_h, eout_h, vocab_h, guid_h,
    out_ref,
    st_v, len_v, sink_v, sinkf_v, k_v, v_v, qkv_v, outw_v, ids_v, rw_v, ein_v, eout_v, voc_v, gd_v,
    send1, recv1, rz, send3, recv3, send4, recv4, send5, recv5, uz, send7, recv7, send8, recv8,
    local_sem, send_sem, recv_sem,
):
    g = lax.axis_index("guide")
    d = lax.axis_index("dp")
    m = lax.axis_index("mp")
    me = g * ND + d

    loads = {}

    def load(name, src, dst):
        copy = pltpu.make_async_copy(src, dst, local_sem.at[len(loads)])
        loads[name] = copy
        copy.start()

    load("states", states_h.at[0], st_v)
    load("lengths", lengths_h, len_v)
    for t in range(3):
        load("qkv%d" % t, qkv_h.at[t], qkv_v.at[:, pl.ds(t * HD, HD)])
    load("sink", sink_h.at[0, :, 0], sink_v)
    load("k", window_h.at[0, :, 0, 0], k_v)
    load("v", window_h.at[0, :, 0, 1], v_v)
    load("outw", outw_h.at[0], outw_v)
    load("ids", ids_h, ids_v)
    load("route", route_h, rw_v)
    load("ein0", ein_h.at[0], ein_v.at[:, pl.ds(0, HD)])
    load("ein1", ein_h.at[1], ein_v.at[:, pl.ds(HD, HD)])
    load("eout", eout_h, eout_v)
    half_start = pl.multiple_of(lax.rem(d, 2) * 64, 64)
    other_start = pl.multiple_of((1 - lax.rem(d, 2)) * 64, 64)
    load("voc0", vocab_h.at[:, pl.ds(0, WIDE)], voc_v.at[0, pl.ds(half_start, 64), :])
    load("voc1", vocab_h.at[:, pl.ds(768, WIDE)], voc_v.at[1, pl.ds(half_start, 64), :])
    load("guid", guid_h, gd_v)

    barrier = pltpu.get_barrier_semaphore()

    def plane_peer(i):
        k = lax.rem(me + i, NP)
        return k, (k // ND, lax.rem(k, ND), m)

    def z_peer(i):
        k = lax.rem(m + i, NZ)
        return k, (g, d, k)

    def greet_z(i, carry):
        pl.semaphore_signal(barrier, inc=1, device_id=z_peer(i)[1], device_id_type=MESH)
        return carry

    def greet_plane(i, carry):
        pl.semaphore_signal(barrier, inc=1, device_id=plane_peer(i)[1], device_id_type=MESH)
        return carry

    lax.fori_loop(1, NZ, greet_z, 0)
    lax.fori_loop(1, NP, greet_plane, 0)

    def remote(phase, src, dst, device):
        pltpu.make_async_remote_copy(
            src_ref=src, dst_ref=dst, send_sem=send_sem.at[phase], recv_sem=recv_sem.at[phase],
            device_id=device, device_id_type=MESH,
        ).start()

    def arrived(phase, ref):
        pltpu.make_async_copy(ref, ref, recv_sem.at[phase]).wait()

    def sent(phase, ref):
        pltpu.make_async_copy(ref, ref, send_sem.at[phase]).wait()

    step_index = lax.rem(iota((1, HD), 1), HD // 2).astype(F32)
    inverse = jnp.exp(step_index * (-2.0 * math.log(10000.0) / HD))
    loads["lengths"].wait()
    position = column(len_v[...].astype(F32))
    angles = position * inverse
    cosine = jnp.cos(angles)
    sine = jnp.sin(angles)
    sine = jnp.where(iota((R, HD), 1) < HD // 2, -sine, sine)
    loads["states"].wait()
    hidden = st_v[...].astype(F32)
    normed = (hidden * lax.rsqrt(jnp.mean(hidden * hidden, axis=-1, keepdims=True) + EPSILON)).astype(BF16)
    loads["sink"].wait()
    for r in range(R):
        for t in range(2):
            sinkf_v[pl.ds(t * R * SINKS + r * SINKS, SINKS), :] = sink_v[r, t].astype(F32)
    for t in range(3):
        loads["qkv%d" % t].wait()
    projected = dot(normed, qkv_v[...])
    query = projected[:, :HD]
    key = projected[:, HD : 2 * HD]
    query = (query * cosine + pltpu.roll(query, HD // 2, axis=1) * sine).astype(BF16)
    key = (key * cosine + pltpu.roll(key, HD // 2, axis=1) * sine).astype(BF16)
    fresh = projected[:, 2 * HD :].astype(BF16)
    root = 1.0 / math.sqrt(HD)
    sinks = sinkf_v[...].astype(BF16)
    loads["k"].wait()
    window_scores = dot_nt(query, k_v[...].reshape(R * WINDOW, HD)) * root
    sink_scores = dot_nt(query, sinks[: R * SINKS]) * root
    self_scores = jnp.sum(query.astype(F32) * key.astype(F32), axis=1, keepdims=True) * root
    position_i = position.astype(jnp.int32)
    slot = iota((R, R * WINDOW), 1)
    window_ok = (slot // WINDOW == iota((R, R * WINDOW), 0)) & (
        lax.rem(slot, WINDOW) >= SINKS + WINDOW - position_i
    )
    slot = iota((R, R * SINKS), 1)
    sink_ok = (slot // SINKS == iota((R, R * SINKS), 0)) & (lax.rem(slot, SINKS) < position_i)
    window_scores = jnp.where(window_ok, window_scores, NEG)
    sink_scores = jnp.where(sink_ok, sink_scores, NEG)
    highest = jnp.maximum(
        jnp.maximum(
            jnp.max(window_scores, axis=1, keepdims=True), jnp.max(sink_scores, axis=1, keepdims=True)
        ),
        self_scores,
    )
    window_exp = jnp.where(window_ok, jnp.exp(window_scores - highest), 0.0)
    sink_exp = jnp.where(sink_ok, jnp.exp(sink_scores - highest), 0.0)
    self_exp = jnp.exp(self_scores - highest)
    total = jnp.sum(window_exp, axis=1, keepdims=True) + jnp.sum(sink_exp, axis=1, keepdims=True) + self_exp
    scale = 1.0 / total
    window_prob = (window_exp * scale).astype(BF16)
    sink_prob = (sink_exp * scale).astype(BF16)
    self_prob = (self_exp * scale).astype(BF16).astype(F32)
    loads["v"].wait()
    mixture = (
        dot(window_prob, v_v[...].reshape(R * WINDOW, HD))
        + dot(sink_prob, sinks[R * SINKS :])
        + self_prob * fresh.astype(F32)
    ).astype(BF16)
    loads["outw"].wait()
    partial = dot(mixture, outw_v[...])
    for j in range(NZ):
        send1[j] = partial[:, j * HD : (j + 1) * HD].astype(BF16)

    pl.semaphore_wait(barrier, NZ - 1 + NP - 1)

    def send_1(i, carry):
        k, device = z_peer(i)
        remote(0, send1.at[k], recv1.at[i - 1], device)
        return carry

    lax.fori_loop(1, NZ, send_1, 0)

    loads["ids"].wait()
    loads["route"].wait()
    half = m // (NZ // 2)
    own_expert = 2 * me + half
    before = (iota((HD, HD), 0) // R == iota((HD, HD), 1) // R) & (iota((HD, HD), 0) < iota((HD, HD), 1))
    before = jnp.where(before, 1.0, 0.0).astype(BF16)
    coefficients = []
    for s in range(2):
        match = ids_v[s] == own_expert
        chosen = jnp.sum(jnp.where(match, 1.0, 0.0), axis=0, keepdims=True)
        weight = jnp.sum(jnp.where(match, rw_v[s], 0.0), axis=0, keepdims=True)
        rank = dot(jnp.broadcast_to(chosen, (R, HD)).astype(BF16), before)[:1]
        rows, lanes = iota((32, HD), 0), iota((32, HD), 1)
        takes = (lanes // R == rows // 2) & (rank.astype(jnp.int32) == lax.rem(rows, 2)) & (chosen > 0.5)
        coefficients.append(jnp.sum(jnp.where(takes, weight, 0.0), axis=1, keepdims=True))
    coefficient = jnp.concatenate(coefficients, axis=0)

    own_ids = jnp.where(g == 0, ids_v[0], ids_v[1]).astype(F32).astype(BF16)
    pick = jnp.where(iota((HD, 64), 0) == d * R + lax.rem(iota((HD, 64), 1), R), 1.0, 0.0).astype(BF16)
    ids_row = dot(own_ids, pick)
    pick = jnp.where(iota((64, HD), 1) == d * R + lax.rem(iota((64, HD), 0), R), 1.0, 0.0).astype(BF16)
    ids_col = dot_nt(pick, own_ids)
    rows = iota((512, 64), 0)
    cols = iota((512, 64), 1)
    expert = (rows // 16 * 2 + half).astype(F32)
    named = jnp.zeros((512, 64), F32)
    for i in range(8):
        named = jnp.where(expert == ids_row[i : i + 1, :], 1.0, named)
    earlier = (iota((64, 64), 0) // R == iota((64, 64), 1) // R) & (iota((64, 64), 0) < iota((64, 64), 1))
    rank = dot(named.astype(BF16), jnp.where(earlier, 1.0, 0.0).astype(BF16))
    scatter = jnp.where(
        (named > 0.5) & (rank.astype(jnp.int32) == lax.rem(rows // 8, 2)) & (lax.rem(rows, 8) == cols // R), 1.0, 0.0
    ).astype(BF16)
    rows = iota((64, 512), 0)
    cols = iota((64, 512), 1)
    expert = (cols // 16 * 2 + half).astype(F32)
    named = jnp.zeros((64, 512), F32)
    for i in range(8):
        named = jnp.where(expert == ids_col[:, i : i + 1], 1.0, named)
    earlier = (iota((64, 64), 0) // R == iota((64, 64), 1) // R) & (iota((64, 64), 1) < iota((64, 64), 0))
    rank = dot(jnp.where(earlier, 1.0, 0.0).astype(BF16), named.astype(BF16))
    gather = jnp.where(
        (named > 0.5) & (rank.astype(jnp.int32) == lax.rem(cols // 8, 2)) & (lax.rem(cols, 8) == rows // R), 1.0, 0.0
    ).astype(BF16)
    rows, cols = iota((64, 64), 0), iota((64, 64), 1)
    swap = jnp.where((rows // 8 == lax.rem(cols, 8)) & (lax.rem(rows, 8) == cols // 8), 1.0, 0.0).astype(BF16)
    voc_v[:, pl.ds(other_start, 64), :] = jnp.zeros((2, 64, WIDE), BF16)

    own_partial = send1[m].astype(F32)
    own_states = st_v[:, pl.ds(pl.multiple_of(m * HD, HD), HD)].astype(F32)
    arrived(0, recv1)
    summed = own_partial + jnp.sum(recv1[...].astype(F32), axis=0)
    residual_chunk = (own_states + summed).astype(BF16)
    rz[m] = residual_chunk

    def send_2(i, carry):
        k, device = z_peer(i)
        remote(1, rz.at[m], rz.at[m], device)
        return carry

    lax.fori_loop(1, NZ, send_2, 0)
    arrived(1, rz.at[pl.ds(0, NZ - 1)])
    pieces = [
        jnp.concatenate([rz[2 * q].astype(F32), rz[2 * q + 1].astype(F32)], axis=1) for q in range(8)
    ]
    squares = sum(jnp.sum(p * p, axis=1, keepdims=True) for p in pieces)
    inv = lax.rsqrt(squares / D + EPSILON)
    stacked = jnp.concatenate([p * inv for p in pieces], axis=0).astype(BF16)

    send3[...] = dot(scatter, stacked).astype(BF16).reshape(NP, 16, 256)

    def send_3(i, carry):
        k, device = plane_peer(i)
        remote(2, send3.at[k], recv3.at[me], device)
        return carry

    lax.fori_loop(1, NP, send_3, 0)
    recv3[me] = send3[me]
    for name in ("ein0", "ein1", "eout"):
        loads[name].wait()
    arrived(2, recv3.at[pl.ds(0, NP - 1)])
    tokens = []
    for n in range(8):
        turned = dot(swap, recv3[4 * n : 4 * n + 4].reshape(64, 256))
        tokens.append(jnp.concatenate([turned[8 * q : 8 * q + 8] for q in range(8)], axis=1))
    tokens = jnp.concatenate(tokens, axis=0).astype(BF16)
    both = dot(tokens, ein_v[...])
    gate, upward = both[:, :HD], both[:, HD:]
    activated = (gate / (1.0 + jnp.exp(-gate)) * upward * coefficient).astype(BF16)
    terms = dot(activated, eout_v[...])
    for n in range(8):
        part = terms[8 * n : 8 * n + 8]
        part = jnp.concatenate([part[:, 256 * q : 256 * q + 256] for q in range(8)], axis=0).astype(BF16)
        send4[4 * n : 4 * n + 4] = dot(swap, part).astype(BF16).reshape(4, 16, 256)

    def send_4(i, carry):
        k, device = plane_peer(i)
        remote(3, send4.at[k], recv4.at[me], device)
        return carry

    lax.fori_loop(1, NP, send_4, 0)
    recv4[me] = send4[me]
    arrived(3, recv4.at[pl.ds(0, NP - 1)])
    own_terms = dot(gather, recv4[...].reshape(512, 256))
    for j in range(NZ):
        send5[j] = own_terms[j // 2 * 8 : j // 2 * 8 + 8, j % 2 * HD : j % 2 * HD + HD].astype(BF16)

    def send_5(i, carry):
        k, device = z_peer(i)
        remote(4, send5.at[k], recv5.at[i - 1], device)
        return carry

    lax.fori_loop(1, NZ, send_5, 0)
    own_sum = residual_chunk.astype(F32) + send5[m].astype(F32)
    arrived(4, recv5)
    uz[m] = (own_sum + jnp.sum(recv5[...].astype(F32), axis=0)).astype(BF16)

    def send_6(i, carry):
        k, device = z_peer(i)
        remote(5, uz.at[m], uz.at[m], device)
        return carry

    lax.fori_loop(1, NZ, send_6, 0)
    loads["guid"].wait()
    guidance = column(gd_v[...])
    share = jnp.where(g == 0, guidance, 1.0 - guidance)
    arrived(5, uz.at[pl.ds(0, NZ - 1)])
    pieces = [uz[j].astype(F32) for j in range(NZ)]
    squares = sum(jnp.sum(p * p, axis=1, keepdims=True) for p in pieces)
    inv = lax.rsqrt(squares / D + EPSILON)
    for j in range(NZ):
        send7[j] = (pieces[j] * inv).astype(BF16).astype(F32) * share

    def send_7(i, carry):
        k, device = plane_peer(i)
        remote(6, send7.at[k // 2], recv7.at[me], device)
        return carry

    lax.fori_loop(1, NP, send_7, 0)
    recv7[me] = send7[me // 2]
    loads["voc0"].wait()
    loads["voc1"].wait()
    arrived(6, recv7.at[pl.ds(0, NP - 1)])
    mixed = (recv7[:ND] + recv7[ND:]).reshape(ND * R, HD).astype(BF16)
    for c in range(2):
        send8[c * ND : (c + 1) * ND] = dot(mixed, voc_v[c]).reshape(ND, R, WIDE).astype(BF16)

    def send_8(i, carry):
        k, device = plane_peer(i)
        remote(7, send8.at[k], recv8.at[me], device)
        return carry

    lax.fori_loop(1, NP, send_8, 0)
    recv8[me] = send8[me]
    arrived(7, recv8.at[pl.ds(0, NP - 1)])
    logits = jnp.sum(recv8[...].astype(F32), axis=0)
    logits = jnp.where(g == 0, logits, pltpu.roll(logits, WIDE - 64, axis=1))
    out_ref[...] = logits[:, :HALF]

    sent(0, recv1)
    sent(1, recv1)
    sent(2, recv3.at[pl.ds(0, NP - 1)])
    sent(3, recv4.at[pl.ds(0, NP - 1)])
    sent(4, recv5)
    sent(5, recv5)
    sent(6, recv7.at[pl.ds(0, NP - 1)])
    sent(7, recv8.at[pl.ds(0, NP - 1)])


def body(
    states, lengths, sink_cache, window_cache, qkv_weight, out_weight, expert_ids, route_weight,
    expert_in, expert_out, vocab_weight, guidance,
):
    qkv = jnp.transpose(qkv_weight, (1, 2, 0, 3)).reshape(3, D, HD)
    ids = jnp.transpose(expert_ids, (0, 2, 1))
    route = jnp.transpose(route_weight, (0, 2, 1))
    guided = pl.pallas_call(
        kernel,
        out_shape=jax.ShapeDtypeStruct((R, HALF), F32),
        in_specs=[pl.BlockSpec(memory_space=pl.ANY)] * 12,
        out_specs=pl.BlockSpec(memory_space=pltpu.VMEM),
        scratch_shapes=[
            pltpu.VMEM((R, D), BF16),
            pltpu.VMEM((1, R), jnp.int32),
            pltpu.VMEM((R, 2, SINKS, HD), BF16),
            pltpu.VMEM((2 * R * SINKS, HD), F32),
            pltpu.VMEM((R, WINDOW, HD), BF16),
            pltpu.VMEM((R, WINDOW, HD), BF16),
            pltpu.VMEM((D, 3 * HD), BF16),
            pltpu.VMEM((HD, D), BF16),
            pltpu.VMEM((2, 8, HD), jnp.int32),
            pltpu.VMEM((2, 8, HD), F32),
            pltpu.VMEM((D, 2 * HD), BF16),
            pltpu.VMEM((HD, D), BF16),
            pltpu.VMEM((2, HD, WIDE), BF16),
            pltpu.VMEM((1, R), F32),
            pltpu.VMEM((NZ, R, HD), BF16),
            pltpu.VMEM((NZ - 1, R, HD), BF16),
            pltpu.VMEM((NZ, R, HD), BF16),
            pltpu.VMEM((NP, 16, 256), BF16),
            pltpu.VMEM((NP, 16, 256), BF16),
            pltpu.VMEM((NP, 16, 256), BF16),
            pltpu.VMEM((NP, 16, 256), BF16),
            pltpu.VMEM((NZ, R, HD), BF16),
            pltpu.VMEM((NZ - 1, R, HD), BF16),
            pltpu.VMEM((NZ, R, HD), BF16),
            pltpu.VMEM((NZ, R, HD), F32),
            pltpu.VMEM((NP, R, HD), F32),
            pltpu.VMEM((NP, R, WIDE), BF16),
            pltpu.VMEM((NP, R, WIDE), BF16),
            pltpu.SemaphoreType.DMA((17,)),
            pltpu.SemaphoreType.DMA((8,)),
            pltpu.SemaphoreType.DMA((8,)),
        ],
        compiler_params=pltpu.CompilerParams(
            collective_id=0, has_side_effects=True, vmem_limit_bytes=56 << 20
        ),
    )(
        states, lengths, sink_cache, window_cache, qkv, out_weight, ids, route,
        expert_in, expert_out, vocab_weight, guidance.reshape(1, R),
    )
    return guided.reshape(R, 1, 1, HALF)


def solution(mesh):
    in_specs = (
        P("guide", "dp", None),
        P("guide", "dp"),
        P("guide", "dp", "mp", None, None, None),
        P("guide", "dp", "mp", None, None, None),
        P(None, None, "mp", None),
        P("mp", None, None),
        P(),
        P(),
        P(None, None, ("guide", "dp", "mp")),
        P(("guide", "dp", "mp"), None),
        P(("guide", "dp"), "mp"),
        P("dp"),
    )
    out_specs = P("dp", "mp", "guide", None)
    return jax.shard_map(body, mesh=mesh, in_specs=in_specs, out_specs=out_specs, check_vma=False)
```

time: 658 us -> 76.4 us (0.12)
  waiting for transfers between devices: 618 us -> 0 us
  Pallas kernels: 0 us -> 74.9 us
  between operations: 14.4 us -> 0.01 us
  matrix products: 9.92 us -> 0 us
  other arithmetic: 9.7 us -> 0 us
    psum x2 -> x0, waiting for transfers between devices: 254 us -> none  [the longest x1 128 us: body(): attention_out = lax.psum(partial_out, 'mp')]
    unnamed x7 -> x0, waiting for transfers between devices: 133 us -> none
    all_gather x2 -> x0, waiting for transfers between devices: 131 us -> none  [the longest x1 65.8 us: body(): final_all = lax.all_gather(final, ('guide', 'dp'), axis=0, tiled=True)]
    reduce_scatter x1 -> x0, waiting for transfers between devices: 99.4 us -> none  [body(): lax.psum_scatter(expert_terms, ('guide', 'dp'), scatter_dimension=0, tile...]
    pallas_call x0 -> x1, Pallas kernels: none -> 74.9 us  [body(): pl.pallas_call(kernel, out_shape=jax.ShapeDtypeStruct((R, HALF), F32), in...]
    dot_general x9 -> x0, matrix products: 9.92 us -> none  [the longest x1 3.17 us: body(): jnp.dot(activated, expert_out, preferred_element_type=jnp.float32)]
  transfers between devices with their start and end apart: 7 -> 0, of which waited for: 7 -> 0; matrix products, arithmetic and copies ran while one was open for 0% -> 0% of each run, Pallas kernels for 0% -> 0%
where the time goes in v1:
time: 76.4 us; the launch traced here: 76.3 us
  Pallas kernels  74.9 us (98%)
  local copies, waits for them, and re-layouts  1.39 us (2%)
    pallas_call x1, Pallas kernels, body(): pl.pallas_call(kernel, out_shape=jax.ShapeDtypeStruct((R, HALF), F32), in...  74.9 us

profile of v1, /device:TPU:1, one launch (start us, length us, event | category | flops | bytes accessed | tf_op | source)
XLA Modules:
  0.0 76.3 jit_solution(5691246358137938213)
XLA Ops:
  0.0 74.9 %shard_map.118 = f32[8,832]{1,0:T(8,128)} custom-call(bf16[1,8,2048]{2,1,0:T(8,128)(2,1)} %states_h.1, s32[1,8]{1,0:T(1,128)} %lengths_h.1, bf16[1,8,1,2,4,128]{5,4,3,2,1,0:T(4,128)(2,1)} %sink_h.1, bf16[1,8,1,2,256,128]{5,4,3,2,1,0:T(8,128)(2,1)} %window_h.1, bf16[3,2048,128]{2,1,0:T(8,128)(2,1)} %bitcast.9, bf16[1,128,2048]{2,1,0:T(8,128)(2,1)} %outw_h.1, ...), custom_call_target="tpu_custom_call" | custom-call | tf_op jit(solution)/shard_map/pallas_call | solution.py:363
  74.9 1.4 %copy.14 = f32[8,1,1,832]{3,2,1,0:T(1,128)} copy(f32[8,1,1,832]{3,0,2,1:T(8,128)} %bitcast.10) | data formatting | bytes 53248 | tf_op jit(solution)/shard_map/reshape | solution.py:408

commit v2 on v1

--- a/solution.py
+++ b/solution.py
@@ -17,6 +17,7 @@
 NZ = 16
 ND = 16
 NP = 32
+NC = 8
 SINKS = 4
 WINDOW = 256
 HALF = 832
@@ -52,6 +53,56 @@
     d = lax.axis_index("dp")
     m = lax.axis_index("mp")
     me = g * ND + d
+
+    barrier = pltpu.get_barrier_semaphore()
+
+    y, x = d // 4, lax.rem(d, 4)
+
+    def turn(a):
+        return jnp.where(a == 0, 2, jnp.where(a == 1, 1, jnp.where(a == 2, 3, 0)))
+
+    def chip(i):
+        return lax.rem(y + turn(i // 4), 4) * 4 + lax.rem(x + turn(lax.rem(i, 4)), 4)
+
+    def to_chips(act):
+        def step(i, carry):
+            other = chip(i)
+            act(g, other)
+            return carry
+
+        lax.fori_loop(0, ND - 1, step, 0)
+
+    def to_plane(act):
+        def step(i, carry):
+            other = chip(i)
+            act(0, other)
+            act(1, other)
+            return carry
+
+        lax.fori_loop(0, ND - 1, step, 0)
+        act(1 - g, d)
+
+    def to_mp(act):
+        def step(i, carry):
+            offset = jnp.where(lax.rem(i, 2) == 0, 8 + i // 2, 8 - (i + 1) // 2)
+            act(lax.rem(m + offset, NZ))
+            return carry
+
+        lax.fori_loop(0, NZ - 1, step, 0)
+
+    def to_near_mp(act):
+        def step(i, carry):
+            offset = jnp.where(lax.rem(i, 2) == 0, 4 - i // 2, 13 + i // 2)
+            act(lax.rem(m + offset, NZ))
+            return carry
+
+        lax.fori_loop(0, NC - 1, step, 0)
+
+    def greet(device):
+        pl.semaphore_signal(barrier, inc=1, device_id=device, device_id_type=MESH)
+
+    to_mp(lambda k: greet((g, d, k)))
+    to_plane(lambda p, q: greet((p, q, m)))
 
     loads = {}
 
@@ -73,32 +124,10 @@
     load("ein0", ein_h.at[0], ein_v.at[:, pl.ds(0, HD)])
     load("ein1", ein_h.at[1], ein_v.at[:, pl.ds(HD, HD)])
     load("eout", eout_h, eout_v)
-    half_start = pl.multiple_of(lax.rem(d, 2) * 64, 64)
-    other_start = pl.multiple_of((1 - lax.rem(d, 2)) * 64, 64)
-    load("voc0", vocab_h.at[:, pl.ds(0, WIDE)], voc_v.at[0, pl.ds(half_start, 64), :])
-    load("voc1", vocab_h.at[:, pl.ds(768, WIDE)], voc_v.at[1, pl.ds(half_start, 64), :])
+    own_columns = pl.ds(pl.multiple_of(g * 768, HD), WIDE)
+    own_rows = pl.ds(pl.multiple_of(g * 64, 64), 64)
+    load("vocab", vocab_h.at[:, own_columns], voc_v.at[own_rows, :])
     load("guid", guid_h, gd_v)
-
-    barrier = pltpu.get_barrier_semaphore()
-
-    def plane_peer(i):
-        k = lax.rem(me + i, NP)
-        return k, (k // ND, lax.rem(k, ND), m)
-
-    def z_peer(i):
-        k = lax.rem(m + i, NZ)
-        return k, (g, d, k)
-
-    def greet_z(i, carry):
-        pl.semaphore_signal(barrier, inc=1, device_id=z_peer(i)[1], device_id_type=MESH)
-        return carry
-
-    def greet_plane(i, carry):
-        pl.semaphore_signal(barrier, inc=1, device_id=plane_peer(i)[1], device_id_type=MESH)
-        return carry
-
-    lax.fori_loop(1, NZ, greet_z, 0)
-    lax.fori_loop(1, NP, greet_plane, 0)
 
     def remote(phase, src, dst, device):
         pltpu.make_async_remote_copy(
@@ -172,17 +201,15 @@
     ).astype(BF16)
     loads["outw"].wait()
     partial = dot(mixture, outw_v[...])
-    for j in range(NZ):
-        send1[j] = partial[:, j * HD : (j + 1) * HD].astype(BF16)
+    for j in range(NC):
+        send1[j] = partial[:, j * 256 : (j + 1) * 256].astype(BF16)
+    chunk = lax.rem(m, NC)
 
     pl.semaphore_wait(barrier, NZ - 1 + NP - 1)
 
-    def send_1(i, carry):
-        k, device = z_peer(i)
-        remote(0, send1.at[k], recv1.at[i - 1], device)
-        return carry
-
-    lax.fori_loop(1, NZ, send_1, 0)
+    to_mp(lambda k: remote(0, send1.at[lax.rem(k, NC)], recv1.at[m], (g, d, k)))
+    recv1[m] = send1[chunk]
+    remote(8, vocab_h.at[:, pl.ds(pl.multiple_of((1 - g) * 768, HD), WIDE)], voc_v.at[own_rows, :], (1 - g, d, m))
 
     loads["ids"].wait()
     loads["route"].wait()
@@ -230,37 +257,22 @@
     ).astype(BF16)
     rows, cols = iota((64, 64), 0), iota((64, 64), 1)
     swap = jnp.where((rows // 8 == lax.rem(cols, 8)) & (lax.rem(rows, 8) == cols // 8), 1.0, 0.0).astype(BF16)
-    voc_v[:, pl.ds(other_start, 64), :] = jnp.zeros((2, 64, WIDE), BF16)
-
-    own_partial = send1[m].astype(F32)
-    own_states = st_v[:, pl.ds(pl.multiple_of(m * HD, HD), HD)].astype(F32)
-    arrived(0, recv1)
-    summed = own_partial + jnp.sum(recv1[...].astype(F32), axis=0)
-    residual_chunk = (own_states + summed).astype(BF16)
-    rz[m] = residual_chunk
-
-    def send_2(i, carry):
-        k, device = z_peer(i)
-        remote(1, rz.at[m], rz.at[m], device)
-        return carry
-
-    lax.fori_loop(1, NZ, send_2, 0)
-    arrived(1, rz.at[pl.ds(0, NZ - 1)])
-    pieces = [
-        jnp.concatenate([rz[2 * q].astype(F32), rz[2 * q + 1].astype(F32)], axis=1) for q in range(8)
-    ]
+
+    own_states = st_v[:, pl.ds(pl.multiple_of(chunk * 256, 256), 256)].astype(F32)
+    arrived(0, recv1.at[pl.ds(0, NZ - 1)])
+    residual_chunk = (own_states + jnp.sum(recv1[...].astype(F32), axis=0)).astype(BF16)
+    rz[chunk] = residual_chunk
+
+    to_near_mp(lambda k: remote(1, rz.at[chunk], rz.at[chunk], (g, d, k)))
+    arrived(1, rz.at[pl.ds(0, NC - 1)])
+    pieces = [rz[q].astype(F32) for q in range(NC)]
     squares = sum(jnp.sum(p * p, axis=1, keepdims=True) for p in pieces)
     inv = lax.rsqrt(squares / D + EPSILON)
     stacked = jnp.concatenate([p * inv for p in pieces], axis=0).astype(BF16)
 
     send3[...] = dot(scatter, stacked).astype(BF16).reshape(NP, 16, 256)
 
-    def send_3(i, carry):
-        k, device = plane_peer(i)
-        remote(2, send3.at[k], recv3.at[me], device)
-        return carry
-
-    lax.fori_loop(1, NP, send_3, 0)
+    to_plane(lambda p, q: remote(2, send3.at[p * ND + q], recv3.at[me], (p, q, m)))
     recv3[me] = send3[me]
     for name in ("ein0", "ein1", "eout"):
         loads[name].wait()
@@ -279,78 +291,59 @@
         part = jnp.concatenate([part[:, 256 * q : 256 * q + 256] for q in range(8)], axis=0).astype(BF16)
         send4[4 * n : 4 * n + 4] = dot(swap, part).astype(BF16).reshape(4, 16, 256)
 
-    def send_4(i, carry):
-        k, device = plane_peer(i)
-        remote(3, send4.at[k], recv4.at[me], device)
-        return carry
-
-    lax.fori_loop(1, NP, send_4, 0)
+    to_plane(lambda p, q: remote(3, send4.at[p * ND + q], recv4.at[me], (p, q, m)))
     recv4[me] = send4[me]
     arrived(3, recv4.at[pl.ds(0, NP - 1)])
     own_terms = dot(gather, recv4[...].reshape(512, 256))
-    for j in range(NZ):
-        send5[j] = own_terms[j // 2 * 8 : j // 2 * 8 + 8, j % 2 * HD : j % 2 * HD + HD].astype(BF16)
-
-    def send_5(i, carry):
-        k, device = z_peer(i)
-        remote(4, send5.at[k], recv5.at[i - 1], device)
-        return carry
-
-    lax.fori_loop(1, NZ, send_5, 0)
-    own_sum = residual_chunk.astype(F32) + send5[m].astype(F32)
-    arrived(4, recv5)
-    uz[m] = (own_sum + jnp.sum(recv5[...].astype(F32), axis=0)).astype(BF16)
-
-    def send_6(i, carry):
-        k, device = z_peer(i)
-        remote(5, uz.at[m], uz.at[m], device)
-        return carry
-
-    lax.fori_loop(1, NZ, send_6, 0)
+    for j in range(NC):
+        send5[j] = own_terms[8 * j : 8 * j + 8].astype(BF16)
+
+    to_mp(lambda k: remote(4, send5.at[lax.rem(k, NC)], recv5.at[m], (g, d, k)))
+    recv5[m] = send5[chunk]
+    arrived(4, recv5.at[pl.ds(0, NZ - 1)])
+    uz[chunk] = (residual_chunk.astype(F32) + jnp.sum(recv5[...].astype(F32), axis=0)).astype(BF16)
+
+    to_near_mp(lambda k: remote(5, uz.at[chunk], uz.at[chunk], (g, d, k)))
     loads["guid"].wait()
     guidance = column(gd_v[...])
     share = jnp.where(g == 0, guidance, 1.0 - guidance)
-    arrived(5, uz.at[pl.ds(0, NZ - 1)])
-    pieces = [uz[j].astype(F32) for j in range(NZ)]
+    low = iota((R, HD), 1) < 64
+    arrived(5, uz.at[pl.ds(0, NC - 1)])
+    pieces = [uz[j].astype(F32) for j in range(NC)]
     squares = sum(jnp.sum(p * p, axis=1, keepdims=True) for p in pieces)
     inv = lax.rsqrt(squares / D + EPSILON)
-    for j in range(NZ):
-        send7[j] = (pieces[j] * inv).astype(BF16).astype(F32) * share
-
-    def send_7(i, carry):
-        k, device = plane_peer(i)
-        remote(6, send7.at[k // 2], recv7.at[me], device)
-        return carry
-
-    lax.fori_loop(1, NP, send_7, 0)
-    recv7[me] = send7[me // 2]
-    loads["voc0"].wait()
-    loads["voc1"].wait()
+    finals = [(p * inv).astype(BF16).astype(F32) * share for p in pieces]
+    finals = [finals[j // 2][:, j % 2 * HD : j % 2 * HD + HD] for j in range(NZ)]
+    for j in range(NC):
+        first, second = finals[j], finals[j + NC]
+        send7[2 * j] = jnp.where(low, first, pltpu.roll(second, 64, axis=1))
+        send7[2 * j + 1] = jnp.where(low, pltpu.roll(first, 64, axis=1), second)
+
+    to_plane(lambda p, q: remote(6, send7.at[q], recv7.at[me], (p, q, m)))
+    recv7[me] = send7[d]
+    loads["vocab"].wait()
+    arrived(8, voc_v.at[pl.ds(0, 64), :])
     arrived(6, recv7.at[pl.ds(0, NP - 1)])
     mixed = (recv7[:ND] + recv7[ND:]).reshape(ND * R, HD).astype(BF16)
-    for c in range(2):
-        send8[c * ND : (c + 1) * ND] = dot(mixed, voc_v[c]).reshape(ND, R, WIDE).astype(BF16)
-
-    def send_8(i, carry):
-        k, device = plane_peer(i)
-        remote(7, send8.at[k], recv8.at[me], device)
-        return carry
-
-    lax.fori_loop(1, NP, send_8, 0)
-    recv8[me] = send8[me]
-    arrived(7, recv8.at[pl.ds(0, NP - 1)])
+    send8[...] = dot(mixed, voc_v[...]).reshape(ND, R, WIDE).astype(BF16)
+
+    to_chips(lambda p, q: remote(7, send8.at[q], recv8.at[d], (p, q, m)))
+    recv8[d] = send8[d]
+    arrived(7, recv8.at[pl.ds(0, ND - 1)])
     logits = jnp.sum(recv8[...].astype(F32), axis=0)
     logits = jnp.where(g == 0, logits, pltpu.roll(logits, WIDE - 64, axis=1))
-    out_ref[...] = logits[:, :HALF]
-
-    sent(0, recv1)
-    sent(1, recv1)
+    for r in range(R):
+        out_ref[r] = logits[r : r + 1, :HALF]
+
+    sent(0, recv1.at[pl.ds(0, NZ - 1)])
+    sent(1, rz.at[pl.ds(0, NC - 1)])
     sent(2, recv3.at[pl.ds(0, NP - 1)])
     sent(3, recv4.at[pl.ds(0, NP - 1)])
-    sent(4, recv5)
-    sent(5, recv5)
+    sent(4, recv5.at[pl.ds(0, NZ - 1)])
+    sent(5, uz.at[pl.ds(0, NC - 1)])
     sent(6, recv7.at[pl.ds(0, NP - 1)])
-    sent(7, recv8.at[pl.ds(0, NP - 1)])
+    sent(7, recv8.at[pl.ds(0, ND - 1)])
+    sent(8, voc_v.at[pl.ds(0, 64), :])
 
 
 def body(
@@ -362,7 +355,7 @@
     route = jnp.transpose(route_weight, (0, 2, 1))
     guided = pl.pallas_call(
         kernel,
-        out_shape=jax.ShapeDtypeStruct((R, HALF), F32),
+        out_shape=jax.ShapeDtypeStruct((R, 1, HALF), F32),
         in_specs=[pl.BlockSpec(memory_space=pl.ANY)] * 12,
         out_specs=pl.BlockSpec(memory_space=pltpu.VMEM),
         scratch_shapes=[
@@ -378,25 +371,25 @@
             pltpu.VMEM((2, 8, HD), F32),
             pltpu.VMEM((D, 2 * HD), BF16),
             pltpu.VMEM((HD, D), BF16),
-            pltpu.VMEM((2, HD, WIDE), BF16),
+            pltpu.VMEM((HD, WIDE), BF16),
             pltpu.VMEM((1, R), F32),
-            pltpu.VMEM((NZ, R, HD), BF16),
-            pltpu.VMEM((NZ - 1, R, HD), BF16),
-            pltpu.VMEM((NZ, R, HD), BF16),
+            pltpu.VMEM((NC, R, 256), BF16),
+            pltpu.VMEM((NZ, R, 256), BF16),
+            pltpu.VMEM((NC, R, 256), BF16),
             pltpu.VMEM((NP, 16, 256), BF16),
             pltpu.VMEM((NP, 16, 256), BF16),
             pltpu.VMEM((NP, 16, 256), BF16),
             pltpu.VMEM((NP, 16, 256), BF16),
-            pltpu.VMEM((NZ, R, HD), BF16),
-            pltpu.VMEM((NZ - 1, R, HD), BF16),
-            pltpu.VMEM((NZ, R, HD), BF16),
-            pltpu.VMEM((NZ, R, HD), F32),
+            pltpu.VMEM((NC, R, 256), BF16),
+            pltpu.VMEM((NZ, R, 256), BF16),
+            pltpu.VMEM((NC, R, 256), BF16),
+            pltpu.VMEM((ND, R, HD), F32),
             pltpu.VMEM((NP, R, HD), F32),
-            pltpu.VMEM((NP, R, WIDE), BF16),
-            pltpu.VMEM((NP, R, WIDE), BF16),
-            pltpu.SemaphoreType.DMA((17,)),
-            pltpu.SemaphoreType.DMA((8,)),
-            pltpu.SemaphoreType.DMA((8,)),
+            pltpu.VMEM((ND, R, WIDE), BF16),
+            pltpu.VMEM((ND, R, WIDE), BF16),
+            pltpu.SemaphoreType.DMA((16,)),
+            pltpu.SemaphoreType.DMA((9,)),
+            pltpu.SemaphoreType.DMA((9,)),
         ],
         compiler_params=pltpu.CompilerParams(
             collective_id=0, has_side_effects=True, vmem_limit_bytes=56 << 20

time: 76.4 us -> 66 us (0.86)
  Pallas kernels: 74.9 us -> 64.4 us
    pallas_call x1, Pallas kernels: 74.9 us -> 64.4 us  [body(): pl.pallas_call(kernel, out_shape=jax.ShapeDtypeStruct((R, 1, HALF), F32),...]
    reshape x1 -> x0, local copies, waits for them, and re-layouts: 1.39 us -> none  [body(): return guided.reshape(R, 1, 1, HALF)]
    unnamed x0 -> x1, local copies, waits for them, and re-layouts: none -> 1.37 us
where the time goes in v2:
time: 66 us; the launch traced here: 65.8 us
  Pallas kernels  64.4 us (98%)
  local copies, waits for them, and re-layouts  1.37 us (2%)
    pallas_call x1, Pallas kernels, body(): pl.pallas_call(kernel, out_shape=jax.ShapeDtypeStruct((R, 1, HALF), F32),...  64.4 us
    unnamed x1, local copies, waits for them, and re-layouts  1.37 us

profile of v2, /device:TPU:1, one launch (start us, length us, event | category | flops | bytes accessed | tf_op | source)
XLA Modules:
  0.0 65.8 jit_solution(8184909154581691554)
XLA Ops:
  0.0 64.4 %shard_map.118 = f32[8,1,832]{2,1,0:T(1,128)} custom-call(bf16[1,8,2048]{2,1,0:T(8,128)(2,1)} %states_h.1, s32[1,8]{1,0:T(1,128)} %lengths_h.1, bf16[1,8,1,2,4,128]{5,4,3,2,1,0:T(4,128)(2,1)} %sink_h.1, bf16[1,8,1,2,256,128]{5,4,3,2,1,0:T(8,128)(2,1)} %window_h.1, bf16[3,2048,128]{2,1,0:T(8,128)(2,1)} %bitcast.11, bf16[1,128,2048]{2,1,0:T(8,128)(2,1)} %outw_h.1, ...), custom_call_target="tpu_custom_call" | custom-call | tf_op jit(solution)/shard_map/pallas_call | solution.py:356
  64.4 1.4 %copy.16 = f32[8,1,1,832]{3,2,1,0:T(1,128)} copy(f32[8,1,1,832]{3,2,1,0:T(1,128)} %bitcast.12) | data formatting | bytes 53248

commit v3 on v2

--- a/solution.py
+++ b/solution.py
@@ -46,7 +46,7 @@
     states_h, lengths_h, sink_h, window_h, qkv_h, outw_h, ids_h, route_h, ein_h, eout_h, vocab_h, guid_h,
     out_ref,
     st_v, len_v, sink_v, sinkf_v, k_v, v_v, qkv_v, outw_v, ids_v, rw_v, ein_v, eout_v, voc_v, gd_v,
-    send1, recv1, rz, send3, recv3, send4, recv4, send5, recv5, uz, send7, recv7, send8, recv8,
+    send1, recv1, windows, rz, gsend, grecv, send3, recv3, send4, recv4, send5, recv5, uz, send7, recv7, send8, recv8,
     local_sem, send_sem, recv_sem,
 ):
     g = lax.axis_index("guide")
@@ -101,7 +101,8 @@
     def greet(device):
         pl.semaphore_signal(barrier, inc=1, device_id=device, device_id_type=MESH)
 
-    to_mp(lambda k: greet((g, d, k)))
+    to_near_mp(lambda k: greet((g, d, k)))
+    greet((g, d, lax.rem(m + 12, NZ)))
     to_plane(lambda p, q: greet((p, q, m)))
 
     loads = {}
@@ -205,11 +206,16 @@
         send1[j] = partial[:, j * 256 : (j + 1) * 256].astype(BF16)
     chunk = lax.rem(m, NC)
 
-    pl.semaphore_wait(barrier, NZ - 1 + NP - 1)
-
-    to_mp(lambda k: remote(0, send1.at[lax.rem(k, NC)], recv1.at[m], (g, d, k)))
-    recv1[m] = send1[chunk]
+    pl.semaphore_wait(barrier, NC + NP - 1)
+
+    to_near_mp(lambda k: remote(0, send1.at[lax.rem(k, NC)], recv1.at[chunk], (g, d, k)))
+    recv1[chunk] = send1[chunk]
     remote(8, vocab_h.at[:, pl.ds(pl.multiple_of((1 - g) * 768, HD), WIDE)], voc_v.at[own_rows, :], (1 - g, d, m))
+
+    loads["guid"].wait()
+    gsend[...] = jnp.broadcast_to(column(gd_v[...]), (R, HD))
+    to_chips(lambda p, q: remote(9, gsend, grecv.at[d], (p, q, m)))
+    grecv[d] = gsend[...]
 
     loads["ids"].wait()
     loads["route"].wait()
@@ -258,14 +264,16 @@
     rows, cols = iota((64, 64), 0), iota((64, 64), 1)
     swap = jnp.where((rows // 8 == lax.rem(cols, 8)) & (lax.rem(rows, 8) == cols // 8), 1.0, 0.0).astype(BF16)
 
-    own_states = st_v[:, pl.ds(pl.multiple_of(chunk * 256, 256), 256)].astype(F32)
-    arrived(0, recv1.at[pl.ds(0, NZ - 1)])
-    residual_chunk = (own_states + jnp.sum(recv1[...].astype(F32), axis=0)).astype(BF16)
-    rz[chunk] = residual_chunk
-
-    to_near_mp(lambda k: remote(1, rz.at[chunk], rz.at[chunk], (g, d, k)))
-    arrived(1, rz.at[pl.ds(0, NC - 1)])
-    pieces = [rz[q].astype(F32) for q in range(NC)]
+    arrived(0, recv1.at[pl.ds(0, NC - 1)])
+    windows[m] = jnp.sum(recv1[...].astype(F32), axis=0).astype(BF16)
+
+    to_mp(lambda k: remote(1, windows.at[m], windows.at[m], (g, d, k)))
+    arrived(1, windows.at[pl.ds(0, NZ - 1)])
+    pieces = []
+    for q in range(NC):
+        total = windows[q].astype(F32) + windows[q + NC].astype(F32)
+        rz[q] = (st_v[:, q * 256 : q * 256 + 256].astype(F32) + total).astype(BF16)
+        pieces.append(rz[q].astype(F32))
     squares = sum(jnp.sum(p * p, axis=1, keepdims=True) for p in pieces)
     inv = lax.rsqrt(squares / D + EPSILON)
     stacked = jnp.concatenate([p * inv for p in pieces], axis=0).astype(BF16)
@@ -301,30 +309,30 @@
     to_mp(lambda k: remote(4, send5.at[lax.rem(k, NC)], recv5.at[m], (g, d, k)))
     recv5[m] = send5[chunk]
     arrived(4, recv5.at[pl.ds(0, NZ - 1)])
-    uz[chunk] = (residual_chunk.astype(F32) + jnp.sum(recv5[...].astype(F32), axis=0)).astype(BF16)
+    uz[chunk] = (rz[chunk].astype(F32) + jnp.sum(recv5[...].astype(F32), axis=0)).astype(BF16)
 
     to_near_mp(lambda k: remote(5, uz.at[chunk], uz.at[chunk], (g, d, k)))
-    loads["guid"].wait()
-    guidance = column(gd_v[...])
-    share = jnp.where(g == 0, guidance, 1.0 - guidance)
     low = iota((R, HD), 1) < 64
     arrived(5, uz.at[pl.ds(0, NC - 1)])
     pieces = [uz[j].astype(F32) for j in range(NC)]
     squares = sum(jnp.sum(p * p, axis=1, keepdims=True) for p in pieces)
     inv = lax.rsqrt(squares / D + EPSILON)
-    finals = [(p * inv).astype(BF16).astype(F32) * share for p in pieces]
+    finals = [p * inv for p in pieces]
     finals = [finals[j // 2][:, j % 2 * HD : j % 2 * HD + HD] for j in range(NZ)]
     for j in range(NC):
         first, second = finals[j], finals[j + NC]
-        send7[2 * j] = jnp.where(low, first, pltpu.roll(second, 64, axis=1))
-        send7[2 * j + 1] = jnp.where(low, pltpu.roll(first, 64, axis=1), second)
+        send7[2 * j] = jnp.where(low, first, pltpu.roll(second, 64, axis=1)).astype(BF16)
+        send7[2 * j + 1] = jnp.where(low, pltpu.roll(first, 64, axis=1), second).astype(BF16)
 
     to_plane(lambda p, q: remote(6, send7.at[q], recv7.at[me], (p, q, m)))
     recv7[me] = send7[d]
     loads["vocab"].wait()
     arrived(8, voc_v.at[pl.ds(0, 64), :])
     arrived(6, recv7.at[pl.ds(0, NP - 1)])
-    mixed = (recv7[:ND] + recv7[ND:]).reshape(ND * R, HD).astype(BF16)
+    arrived(9, grecv.at[pl.ds(0, ND - 1)])
+    conditional, unconditional = recv7[:ND].astype(F32), recv7[ND:].astype(F32)
+    mixed = unconditional + grecv[...] * (conditional - unconditional)
+    mixed = mixed.reshape(ND * R, HD).astype(BF16)
     send8[...] = dot(mixed, voc_v[...]).reshape(ND, R, WIDE).astype(BF16)
 
     to_chips(lambda p, q: remote(7, send8.at[q], recv8.at[d], (p, q, m)))
@@ -335,8 +343,8 @@
     for r in range(R):
         out_ref[r] = logits[r : r + 1, :HALF]
 
-    sent(0, recv1.at[pl.ds(0, NZ - 1)])
-    sent(1, rz.at[pl.ds(0, NC - 1)])
+    sent(0, recv1.at[pl.ds(0, NC - 1)])
+    sent(1, windows.at[pl.ds(0, NZ - 1)])
     sent(2, recv3.at[pl.ds(0, NP - 1)])
     sent(3, recv4.at[pl.ds(0, NP - 1)])
     sent(4, recv5.at[pl.ds(0, NZ - 1)])
@@ -344,6 +352,7 @@
     sent(6, recv7.at[pl.ds(0, NP - 1)])
     sent(7, recv8.at[pl.ds(0, ND - 1)])
     sent(8, voc_v.at[pl.ds(0, 64), :])
+    sent(9, grecv.at[pl.ds(0, ND - 1)])
 
 
 def body(
@@ -374,8 +383,11 @@
             pltpu.VMEM((HD, WIDE), BF16),
             pltpu.VMEM((1, R), F32),
             pltpu.VMEM((NC, R, 256), BF16),
+            pltpu.VMEM((NC, R, 256), BF16),
             pltpu.VMEM((NZ, R, 256), BF16),
             pltpu.VMEM((NC, R, 256), BF16),
+            pltpu.VMEM((R, HD), F32),
+            pltpu.VMEM((ND, R, HD), F32),
             pltpu.VMEM((NP, 16, 256), BF16),
             pltpu.VMEM((NP, 16, 256), BF16),
             pltpu.VMEM((NP, 16, 256), BF16),
@@ -383,13 +395,13 @@
             pltpu.VMEM((NC, R, 256), BF16),
             pltpu.VMEM((NZ, R, 256), BF16),
             pltpu.VMEM((NC, R, 256), BF16),
-            pltpu.VMEM((ND, R, HD), F32),
-            pltpu.VMEM((NP, R, HD), F32),
+            pltpu.VMEM((ND, R, HD), BF16),
+            pltpu.VMEM((NP, R, HD), BF16),
             pltpu.VMEM((ND, R, WIDE), BF16),
             pltpu.VMEM((ND, R, WIDE), BF16),
             pltpu.SemaphoreType.DMA((16,)),
-            pltpu.SemaphoreType.DMA((9,)),
-            pltpu.SemaphoreType.DMA((9,)),
+            pltpu.SemaphoreType.DMA((10,)),
+            pltpu.SemaphoreType.DMA((10,)),
         ],
         compiler_params=pltpu.CompilerParams(
             collective_id=0, has_side_effects=True, vmem_limit_bytes=56 << 20

time: 66 us -> 63.8 us (0.967)
  Pallas kernels: 64.4 us -> 62.3 us
    pallas_call x1, Pallas kernels: 64.4 us -> 62.3 us  [body(): pl.pallas_call(kernel, out_shape=jax.ShapeDtypeStruct((R, 1, HALF), F32),...]
where the time goes in v3:
time: 63.8 us; the launch traced here: 63.7 us
  Pallas kernels  62.3 us (98%)
  local copies, waits for them, and re-layouts  1.37 us (2%)
    pallas_call x1, Pallas kernels, body(): pl.pallas_call(kernel, out_shape=jax.ShapeDtypeStruct((R, 1, HALF), F32),...  62.3 us
    unnamed x1, local copies, waits for them, and re-layouts  1.37 us

profile of v3, /device:TPU:1, one launch (start us, length us, event | category | flops | bytes accessed | tf_op | source)
XLA Modules:
  0.0 63.7 jit_solution(12041064958234300173)
XLA Ops:
  0.0 62.3 %shard_map.118 = f32[8,1,832]{2,1,0:T(1,128)} custom-call(bf16[1,8,2048]{2,1,0:T(8,128)(2,1)} %states_h.1, s32[1,8]{1,0:T(1,128)} %lengths_h.1, bf16[1,8,1,2,4,128]{5,4,3,2,1,0:T(4,128)(2,1)} %sink_h.1, bf16[1,8,1,2,256,128]{5,4,3,2,1,0:T(8,128)(2,1)} %window_h.1, bf16[3,2048,128]{2,1,0:T(8,128)(2,1)} %bitcast.11, bf16[1,128,2048]{2,1,0:T(8,128)(2,1)} %outw_h.1, ...), custom_call_target="tpu_custom_call" | custom-call | tf_op jit(solution)/shard_map/pallas_call | solution.py:365
  62.3 1.4 %copy.16 = f32[8,1,1,832]{3,2,1,0:T(1,128)} copy(f32[8,1,1,832]{3,2,1,0:T(1,128)} %bitcast.12) | data formatting | bytes 53248

commit v4 on v3

--- a/solution.py
+++ b/solution.py
@@ -46,7 +46,7 @@
     states_h, lengths_h, sink_h, window_h, qkv_h, outw_h, ids_h, route_h, ein_h, eout_h, vocab_h, guid_h,
     out_ref,
     st_v, len_v, sink_v, sinkf_v, k_v, v_v, qkv_v, outw_v, ids_v, rw_v, ein_v, eout_v, voc_v, gd_v,
-    send1, recv1, windows, rz, gsend, grecv, send3, recv3, send4, recv4, send5, recv5, uz, send7, recv7, send8, recv8,
+    send1, recv1, windows, gather, rsend, rrecv, send3, recv3, send4, recv4, send5, recv5, uz, send8, recv8,
     local_sem, send_sem, recv_sem,
 ):
     g = lax.axis_index("guide")
@@ -212,11 +212,6 @@
     recv1[chunk] = send1[chunk]
     remote(8, vocab_h.at[:, pl.ds(pl.multiple_of((1 - g) * 768, HD), WIDE)], voc_v.at[own_rows, :], (1 - g, d, m))
 
-    loads["guid"].wait()
-    gsend[...] = jnp.broadcast_to(column(gd_v[...]), (R, HD))
-    to_chips(lambda p, q: remote(9, gsend, grecv.at[d], (p, q, m)))
-    grecv[d] = gsend[...]
-
     loads["ids"].wait()
     loads["route"].wait()
     half = m // (NZ // 2)
@@ -237,8 +232,6 @@
     own_ids = jnp.where(g == 0, ids_v[0], ids_v[1]).astype(F32).astype(BF16)
     pick = jnp.where(iota((HD, 64), 0) == d * R + lax.rem(iota((HD, 64), 1), R), 1.0, 0.0).astype(BF16)
     ids_row = dot(own_ids, pick)
-    pick = jnp.where(iota((64, HD), 1) == d * R + lax.rem(iota((64, HD), 0), R), 1.0, 0.0).astype(BF16)
-    ids_col = dot_nt(pick, own_ids)
     rows = iota((512, 64), 0)
     cols = iota((512, 64), 1)
     expert = (rows // 16 * 2 + half).astype(F32)
@@ -250,17 +243,17 @@
     scatter = jnp.where(
         (named > 0.5) & (rank.astype(jnp.int32) == lax.rem(rows // 8, 2)) & (lax.rem(rows, 8) == cols // R), 1.0, 0.0
     ).astype(BF16)
-    rows = iota((64, 512), 0)
-    cols = iota((64, 512), 1)
-    expert = (cols // 16 * 2 + half).astype(F32)
-    named = jnp.zeros((64, 512), F32)
+    eye = jnp.where(iota((HD, HD), 0) == iota((HD, HD), 1), 1.0, 0.0).astype(BF16)
+    ids_col = dot_nt(eye, own_ids)
+    cols = iota((HD, 1024), 1)
+    expert = (cols // 32 * 2 + half).astype(F32)
+    named = jnp.zeros((HD, 1024), F32)
     for i in range(8):
         named = jnp.where(expert == ids_col[:, i : i + 1], 1.0, named)
-    earlier = (iota((64, 64), 0) // R == iota((64, 64), 1) // R) & (iota((64, 64), 1) < iota((64, 64), 0))
+    earlier = (iota((HD, HD), 0) // R == iota((HD, HD), 1) // R) & (iota((HD, HD), 1) < iota((HD, HD), 0))
     rank = dot(jnp.where(earlier, 1.0, 0.0).astype(BF16), named.astype(BF16))
-    gather = jnp.where(
-        (named > 0.5) & (rank.astype(jnp.int32) == lax.rem(cols // 8, 2)) & (lax.rem(cols, 8) == rows // R), 1.0, 0.0
-    ).astype(BF16)
+    takes = (rank.astype(jnp.int32) == lax.rem(cols, 2)) & (lax.rem(cols, 32) // 2 == iota((HD, 1024), 0) // R)
+    gather[...] = jnp.where(takes & (named > 0.5), 1.0, 0.0).astype(BF16)
     rows, cols = iota((64, 64), 0), iota((64, 64), 1)
     swap = jnp.where((rows // 8 == lax.rem(cols, 8)) & (lax.rem(rows, 8) == cols // 8), 1.0, 0.0).astype(BF16)
 
@@ -272,8 +265,7 @@
     pieces = []
     for q in range(NC):
         total = windows[q].astype(F32) + windows[q + NC].astype(F32)
-        rz[q] = (st_v[:, q * 256 : q * 256 + 256].astype(F32) + total).astype(BF16)
-        pieces.append(rz[q].astype(F32))
+        pieces.append((st_v[:, q * 256 : q * 256 + 256].astype(F32) + total).astype(BF16).astype(F32))
     squares = sum(jnp.sum(p * p, axis=1, keepdims=True) for p in pieces)
     inv = lax.rsqrt(squares / D + EPSILON)
     stacked = jnp.concatenate([p * inv for p in pieces], axis=0).astype(BF16)
@@ -282,6 +274,15 @@
 
     to_plane(lambda p, q: remote(2, send3.at[p * ND + q], recv3.at[me], (p, q, m)))
     recv3[me] = send3[me]
+
+    low = iota((R, HD), 1) < 64
+    for j in range(NC):
+        first = pieces[j // 2][:, j % 2 * HD : j % 2 * HD + HD]
+        second = pieces[j // 2 + 4][:, j % 2 * HD : j % 2 * HD + HD]
+        rsend[2 * j] = jnp.where(low, first, pltpu.roll(second, 64, axis=1)).astype(BF16)
+        rsend[2 * j + 1] = jnp.where(low, pltpu.roll(first, 64, axis=1), second).astype(BF16)
+    to_chips(lambda p, q: remote(9, rsend.at[q], rrecv.at[d], (p, q, m)))
+    rrecv[d] = rsend[d]
     for name in ("ein0", "ein1", "eout"):
         loads[name].wait()
     arrived(2, recv3.at[pl.ds(0, NP - 1)])
@@ -294,51 +295,59 @@
     gate, upward = both[:, :HD], both[:, HD:]
     activated = (gate / (1.0 + jnp.exp(-gate)) * upward * coefficient).astype(BF16)
     terms = dot(activated, eout_v[...])
-    for n in range(8):
-        part = terms[8 * n : 8 * n + 8]
-        part = jnp.concatenate([part[:, 256 * q : 256 * q + 256] for q in range(8)], axis=0).astype(BF16)
-        send4[4 * n : 4 * n + 4] = dot(swap, part).astype(BF16).reshape(4, 16, 256)
-
-    to_plane(lambda p, q: remote(3, send4.at[p * ND + q], recv4.at[me], (p, q, m)))
-    recv4[me] = send4[me]
+    low = iota((64, HD), 1) < 64
+    for j in range(NC):
+        first, second = terms[:, j * HD : j * HD + HD], terms[:, (j + NC) * HD : (j + NC) * HD + HD]
+        send4[2 * j] = jnp.where(low, first, pltpu.roll(second, 64, axis=1)).astype(BF16)
+        send4[2 * j + 1] = jnp.where(low, pltpu.roll(first, 64, axis=1), second).astype(BF16)
+
+    to_plane(lambda p, q: remote(3, send4.at[q, pl.ds(pl.multiple_of(p * 32, 32), 32)], recv4.at[me], (p, q, m)))
+    recv4[me] = send4[d, pl.ds(pl.multiple_of(g * 32, 32), 32)]
     arrived(3, recv4.at[pl.ds(0, NP - 1)])
-    own_terms = dot(gather, recv4[...].reshape(512, 256))
-    for j in range(NC):
-        send5[j] = own_terms[8 * j : 8 * j + 8].astype(BF16)
+    send5[...] = dot(gather[...], recv4[...].reshape(1024, HD)).astype(BF16).reshape(NC, 16, HD)
 
     to_mp(lambda k: remote(4, send5.at[lax.rem(k, NC)], recv5.at[m], (g, d, k)))
     recv5[m] = send5[chunk]
+    arrived(9, rrecv.at[pl.ds(0, ND - 1)])
+    residual = rrecv[pl.ds(2 * chunk, 2)].astype(F32).reshape(16, HD)
     arrived(4, recv5.at[pl.ds(0, NZ - 1)])
-    uz[chunk] = (rz[chunk].astype(F32) + jnp.sum(recv5[...].astype(F32), axis=0)).astype(BF16)
-
-    to_near_mp(lambda k: remote(5, uz.at[chunk], uz.at[chunk], (g, d, k)))
-    low = iota((R, HD), 1) < 64
-    arrived(5, uz.at[pl.ds(0, NC - 1)])
-    pieces = [uz[j].astype(F32) for j in range(NC)]
-    squares = sum(jnp.sum(p * p, axis=1, keepdims=True) for p in pieces)
-    inv = lax.rsqrt(squares / D + EPSILON)
-    finals = [p * inv for p in pieces]
-    finals = [finals[j // 2][:, j % 2 * HD : j % 2 * HD + HD] for j in range(NZ)]
-    for j in range(NC):
-        first, second = finals[j], finals[j + NC]
-        send7[2 * j] = jnp.where(low, first, pltpu.roll(second, 64, axis=1)).astype(BF16)
-        send7[2 * j + 1] = jnp.where(low, pltpu.roll(first, 64, axis=1), second).astype(BF16)
-
-    to_plane(lambda p, q: remote(6, send7.at[q], recv7.at[me], (p, q, m)))
-    recv7[me] = send7[d]
+    uz[g, chunk] = (residual + jnp.sum(recv5[...].astype(F32), axis=0)).astype(BF16)
+
+    def send_6(k):
+        remote(5, uz.at[g, chunk], uz.at[g, chunk], (g, d, k))
+        remote(5, uz.at[g, chunk], uz.at[g, chunk], (1 - g, d, k))
+
+    to_near_mp(send_6)
+    remote(5, uz.at[g, chunk], uz.at[g, chunk], (1 - g, d, m))
+    loads["guid"].wait()
+    guidance = column(gd_v[...])
     loads["vocab"].wait()
     arrived(8, voc_v.at[pl.ds(0, 64), :])
-    arrived(6, recv7.at[pl.ds(0, NP - 1)])
-    arrived(9, grecv.at[pl.ds(0, ND - 1)])
-    conditional, unconditional = recv7[:ND].astype(F32), recv7[ND:].astype(F32)
-    mixed = unconditional + grecv[...] * (conditional - unconditional)
-    mixed = mixed.reshape(ND * R, HD).astype(BF16)
-    send8[...] = dot(mixed, voc_v[...]).reshape(ND, R, WIDE).astype(BF16)
+    arrived(5, recv5.at[pl.ds(0, NZ - 1)])
+    sums = uz[...].reshape(2 * ND * R, HD)
+    squares = jnp.sum(sums.astype(F32) * sums.astype(F32), axis=1, keepdims=True)
+    upper = squares.astype(BF16).astype(F32)
+    lanes = iota((2 * ND * R, HD), 1)
+    marks = jnp.where(lax.rem(lanes, 64) < 32, upper, squares - upper)
+    partial = dot(sums, voc_v[...])
+    first = jnp.where((lanes < 64) & (g == 1), marks, partial[:, :HD])
+    last = jnp.where((lanes >= 64) & (g == 0), marks, partial[:, WIDE - HD :])
+    for part, start in ((first, 0), (partial[:, HD : WIDE - HD], HD), (last, WIDE - HD)):
+        part = part.astype(BF16)
+        for t in range(2):
+            send8[:, t * R : t * R + R, start : start + part.shape[1]] = part[t * HD : t * HD + HD].reshape(
+                ND, R, part.shape[1]
+            )
 
     to_chips(lambda p, q: remote(7, send8.at[q], recv8.at[d], (p, q, m)))
     recv8[d] = send8[d]
     arrived(7, recv8.at[pl.ds(0, ND - 1)])
     logits = jnp.sum(recv8[...].astype(F32), axis=0)
+    lanes = iota((2 * R, WIDE), 1)
+    spare = ((lanes < 64) & (g == 1)) | ((lanes >= HALF) & (g == 0))
+    squares = jnp.sum(jnp.where(spare, logits, 0.0), axis=1, keepdims=True) * (1.0 / 32)
+    logits = logits * lax.rsqrt(squares / D + EPSILON)
+    logits = logits[R:] + guidance * (logits[:R] - logits[R:])
     logits = jnp.where(g == 0, logits, pltpu.roll(logits, WIDE - 64, axis=1))
     for r in range(R):
         out_ref[r] = logits[r : r + 1, :HALF]
@@ -348,11 +357,10 @@
     sent(2, recv3.at[pl.ds(0, NP - 1)])
     sent(3, recv4.at[pl.ds(0, NP - 1)])
     sent(4, recv5.at[pl.ds(0, NZ - 1)])
-    sent(5, uz.at[pl.ds(0, NC - 1)])
-    sent(6, recv7.at[pl.ds(0, NP - 1)])
+    sent(5, recv5.at[pl.ds(0, NZ - 1)])
     sent(7, recv8.at[pl.ds(0, ND - 1)])
     sent(8, voc_v.at[pl.ds(0, 64), :])
-    sent(9, grecv.at[pl.ds(0, ND - 1)])
+    sent(9, rrecv.at[pl.ds(0, ND - 1)])
 
 
 def body(
@@ -364,7 +372,7 @@
     route = jnp.transpose(route_weight, (0, 2, 1))
     guided = pl.pallas_call(
         kernel,
-        out_shape=jax.ShapeDtypeStruct((R, 1, HALF), F32),
+        out_shape=pltpu.VMEM((R, 1, HALF), F32),
         in_specs=[pl.BlockSpec(memory_space=pl.ANY)] * 12,
         out_specs=pl.BlockSpec(memory_space=pltpu.VMEM),
         scratch_shapes=[
@@ -385,20 +393,18 @@
             pltpu.VMEM((NC, R, 256), BF16),
             pltpu.VMEM((NC, R, 256), BF16),
             pltpu.VMEM((NZ, R, 256), BF16),
-            pltpu.VMEM((NC, R, 256), BF16),
-            pltpu.VMEM((R, HD), F32),
-            pltpu.VMEM((ND, R, HD), F32),
+            pltpu.VMEM((HD, 1024), BF16),
+            pltpu.VMEM((ND, R, HD), BF16),
+            pltpu.VMEM((ND, R, HD), BF16),
             pltpu.VMEM((NP, 16, 256), BF16),
             pltpu.VMEM((NP, 16, 256), BF16),
-            pltpu.VMEM((NP, 16, 256), BF16),
-            pltpu.VMEM((NP, 16, 256), BF16),
-            pltpu.VMEM((NC, R, 256), BF16),
-            pltpu.VMEM((NZ, R, 256), BF16),
-            pltpu.VMEM((NC, R, 256), BF16),
-            pltpu.VMEM((ND, R, HD), BF16),
-            pltpu.VMEM((NP, R, HD), BF16),
-            pltpu.VMEM((ND, R, WIDE), BF16),
-            pltpu.VMEM((ND, R, WIDE), BF16),
+            pltpu.VMEM((ND, 64, HD), BF16),
+            pltpu.VMEM((NP, 32, HD), BF16),
+            pltpu.VMEM((NC, 16, HD), BF16),
+            pltpu.VMEM((NZ, 16, HD), BF16),
+            pltpu.VMEM((2, NC, 16, HD), BF16),
+            pltpu.VMEM((ND, 16, WIDE), BF16),
+            pltpu.VMEM((ND, 16, WIDE), BF16),
             pltpu.SemaphoreType.DMA((16,)),
             pltpu.SemaphoreType.DMA((10,)),
             pltpu.SemaphoreType.DMA((10,)),

time: 63.8 us -> 59.8 us (0.937)
  Pallas kernels: 62.3 us -> 59.1 us
  local copies, waits for them, and re-layouts: 1.37 us -> 0.61 us
    pallas_call x1, Pallas kernels: 62.3 us -> 59.1 us  [body(): pl.pallas_call(kernel, out_shape=pltpu.VMEM((R, 1, HALF), F32), in_specs=...]
    unnamed x1, local copies, waits for them, and re-layouts: 1.37 us -> 0.61 us
where the time goes in v4:
time: 59.8 us; the launch traced here: 59.7 us
  Pallas kernels  59.1 us (99%)
  local copies, waits for them, and re-layouts  0.61 us (1%)
    pallas_call x1, Pallas kernels, body(): pl.pallas_call(kernel, out_shape=pltpu.VMEM((R, 1, HALF), F32), in_specs=...  59.1 us

profile of v4, /device:TPU:1, one launch (start us, length us, event | category | flops | bytes accessed | tf_op | source)
XLA Modules:
  0.0 59.7 jit_solution(4572691084280258533)
XLA Ops:
  0.0 59.1 %shard_map.118 = f32[8,1,832]{2,1,0:T(1,128)S(1)} custom-call(bf16[1,8,2048]{2,1,0:T(8,128)(2,1)} %states_h.1, s32[1,8]{1,0:T(1,128)} %lengths_h.1, bf16[1,8,1,2,4,128]{5,4,3,2,1,0:T(4,128)(2,1)} %sink_h.1, bf16[1,8,1,2,256,128]{5,4,3,2,1,0:T(8,128)(2,1)} %window_h.1, bf16[3,2048,128]{2,1,0:T(8,128)(2,1)} %bitcast.12, bf16[1,128,2048]{2,1,0:T(8,128)(2,1)} %outw_h.1, ...), custom_call_target="tpu_custom_call" | custom-call | tf_op jit(solution)/shard_map/pallas_call | solution.py:373
  59.1 0.6 %copy.16 = f32[8,1,1,832]{3,2,1,0:T(1,128)} copy(f32[8,1,1,832]{3,2,1,0:T(1,128)S(1)} %bitcast.11) | data formatting | bytes 53248

commit v5 on v4

--- a/solution.py
+++ b/solution.py
@@ -103,7 +103,6 @@
 
     to_near_mp(lambda k: greet((g, d, k)))
     greet((g, d, lax.rem(m + 12, NZ)))
-    to_plane(lambda p, q: greet((p, q, m)))
 
     loads = {}
 
@@ -120,6 +119,7 @@
     load("k", window_h.at[0, :, 0, 0], k_v)
     load("v", window_h.at[0, :, 0, 1], v_v)
     load("outw", outw_h.at[0], outw_v)
+    to_plane(lambda p, q: greet((p, q, m)))
     load("ids", ids_h, ids_v)
     load("route", route_h, rw_v)
     load("ein0", ein_h.at[0], ein_v.at[:, pl.ds(0, HD)])
@@ -243,6 +243,14 @@
     scatter = jnp.where(
         (named > 0.5) & (rank.astype(jnp.int32) == lax.rem(rows // 8, 2)) & (lax.rem(rows, 8) == cols // R), 1.0, 0.0
     ).astype(BF16)
+    rows, cols = iota((64, 64), 0), iota((64, 64), 1)
+    swap = jnp.where((rows // 8 == lax.rem(cols, 8)) & (lax.rem(rows, 8) == cols // 8), 1.0, 0.0).astype(BF16)
+
+    arrived(0, recv1.at[pl.ds(0, NC - 1)])
+    windows[m] = jnp.sum(recv1[...].astype(F32), axis=0).astype(BF16)
+
+    to_mp(lambda k: remote(1, windows.at[m], windows.at[m], (g, d, k)))
+
     eye = jnp.where(iota((HD, HD), 0) == iota((HD, HD), 1), 1.0, 0.0).astype(BF16)
     ids_col = dot_nt(eye, own_ids)
     cols = iota((HD, 1024), 1)
@@ -254,13 +262,6 @@
     rank = dot(jnp.where(earlier, 1.0, 0.0).astype(BF16), named.astype(BF16))
     takes = (rank.astype(jnp.int32) == lax.rem(cols, 2)) & (lax.rem(cols, 32) // 2 == iota((HD, 1024), 0) // R)
     gather[...] = jnp.where(takes & (named > 0.5), 1.0, 0.0).astype(BF16)
-    rows, cols = iota((64, 64), 0), iota((64, 64), 1)
-    swap = jnp.where((rows // 8 == lax.rem(cols, 8)) & (lax.rem(rows, 8) == cols // 8), 1.0, 0.0).astype(BF16)
-
-    arrived(0, recv1.at[pl.ds(0, NC - 1)])
-    windows[m] = jnp.sum(recv1[...].astype(F32), axis=0).astype(BF16)
-
-    to_mp(lambda k: remote(1, windows.at[m], windows.at[m], (g, d, k)))
     arrived(1, windows.at[pl.ds(0, NZ - 1)])
     pieces = []
     for q in range(NC):
@@ -281,8 +282,6 @@
         second = pieces[j // 2 + 4][:, j % 2 * HD : j % 2 * HD + HD]
         rsend[2 * j] = jnp.where(low, first, pltpu.roll(second, 64, axis=1)).astype(BF16)
         rsend[2 * j + 1] = jnp.where(low, pltpu.roll(first, 64, axis=1), second).astype(BF16)
-    to_chips(lambda p, q: remote(9, rsend.at[q], rrecv.at[d], (p, q, m)))
-    rrecv[d] = rsend[d]
     for name in ("ein0", "ein1", "eout"):
         loads[name].wait()
     arrived(2, recv3.at[pl.ds(0, NP - 1)])
@@ -307,6 +306,8 @@
     send5[...] = dot(gather[...], recv4[...].reshape(1024, HD)).astype(BF16).reshape(NC, 16, HD)
 
     to_mp(lambda k: remote(4, send5.at[lax.rem(k, NC)], recv5.at[m], (g, d, k)))
+    to_chips(lambda p, q: remote(9, rsend.at[q], rrecv.at[d], (p, q, m)))
+    rrecv[d] = rsend[d]
     recv5[m] = send5[chunk]
     arrived(9, rrecv.at[pl.ds(0, ND - 1)])
     residual = rrecv[pl.ds(2 * chunk, 2)].astype(F32).reshape(16, HD)

time: 59.8 us -> 60 us (level)
  no operation moved by 1% of the time
where the time goes in v5:
time: 60 us; the launch traced here: 59.9 us
  Pallas kernels  59.3 us (99%)
  local copies, waits for them, and re-layouts  0.61 us (1%)
    pallas_call x1, Pallas kernels, body(): pl.pallas_call(kernel, out_shape=pltpu.VMEM((R, 1, HALF), F32), in_specs=...  59.3 us

profile of v5, /device:TPU:1, one launch (start us, length us, event | category | flops | bytes accessed | tf_op | source)
XLA Modules:
  0.0 59.9 jit_solution(15041667928144569210)
XLA Ops:
  0.0 59.3 %shard_map.118 = f32[8,1,832]{2,1,0:T(1,128)S(1)} custom-call(bf16[1,8,2048]{2,1,0:T(8,128)(2,1)} %states_h.1, s32[1,8]{1,0:T(1,128)} %lengths_h.1, bf16[1,8,1,2,4,128]{5,4,3,2,1,0:T(4,128)(2,1)} %sink_h.1, bf16[1,8,1,2,256,128]{5,4,3,2,1,0:T(8,128)(2,1)} %window_h.1, bf16[3,2048,128]{2,1,0:T(8,128)(2,1)} %bitcast.12, bf16[1,128,2048]{2,1,0:T(8,128)(2,1)} %outw_h.1, ...), custom_call_target="tpu_custom_call" | custom-call | tf_op jit(solution)/shard_map/pallas_call | solution.py:374
  59.3 0.6 %copy.16 = f32[8,1,1,832]{3,2,1,0:T(1,128)} copy(f32[8,1,1,832]{3,2,1,0:T(1,128)S(1)} %bitcast.11) | data formatting | bytes 53248

commit v6 on v4

--- a/solution.py
+++ b/solution.py
@@ -103,7 +103,6 @@
 
     to_near_mp(lambda k: greet((g, d, k)))
     greet((g, d, lax.rem(m + 12, NZ)))
-    to_plane(lambda p, q: greet((p, q, m)))
 
     loads = {}
 
@@ -120,6 +119,7 @@
     load("k", window_h.at[0, :, 0, 0], k_v)
     load("v", window_h.at[0, :, 0, 1], v_v)
     load("outw", outw_h.at[0], outw_v)
+    to_plane(lambda p, q: greet((p, q, m)))
     load("ids", ids_h, ids_v)
     load("route", route_h, rw_v)
     load("ein0", ein_h.at[0], ein_v.at[:, pl.ds(0, HD)])
@@ -281,8 +281,6 @@
         second = pieces[j // 2 + 4][:, j % 2 * HD : j % 2 * HD + HD]
         rsend[2 * j] = jnp.where(low, first, pltpu.roll(second, 64, axis=1)).astype(BF16)
         rsend[2 * j + 1] = jnp.where(low, pltpu.roll(first, 64, axis=1), second).astype(BF16)
-    to_chips(lambda p, q: remote(9, rsend.at[q], rrecv.at[d], (p, q, m)))
-    rrecv[d] = rsend[d]
     for name in ("ein0", "ein1", "eout"):
         loads[name].wait()
     arrived(2, recv3.at[pl.ds(0, NP - 1)])
@@ -307,6 +305,8 @@
     send5[...] = dot(gather[...], recv4[...].reshape(1024, HD)).astype(BF16).reshape(NC, 16, HD)
 
     to_mp(lambda k: remote(4, send5.at[lax.rem(k, NC)], recv5.at[m], (g, d, k)))
+    to_chips(lambda p, q: remote(9, rsend.at[q], rrecv.at[d], (p, q, m)))
+    rrecv[d] = rsend[d]
     recv5[m] = send5[chunk]
     arrived(9, rrecv.at[pl.ds(0, ND - 1)])
     residual = rrecv[pl.ds(2 * chunk, 2)].astype(F32).reshape(16, HD)
@@ -324,30 +324,31 @@
     loads["vocab"].wait()
     arrived(8, voc_v.at[pl.ds(0, 64), :])
     arrived(5, recv5.at[pl.ds(0, NZ - 1)])
-    sums = uz[...].reshape(2 * ND * R, HD)
-    squares = jnp.sum(sums.astype(F32) * sums.astype(F32), axis=1, keepdims=True)
-    upper = squares.astype(BF16).astype(F32)
-    lanes = iota((2 * ND * R, HD), 1)
-    marks = jnp.where(lax.rem(lanes, 64) < 32, upper, squares - upper)
-    partial = dot(sums, voc_v[...])
-    first = jnp.where((lanes < 64) & (g == 1), marks, partial[:, :HD])
-    last = jnp.where((lanes >= 64) & (g == 0), marks, partial[:, WIDE - HD :])
-    for part, start in ((first, 0), (partial[:, HD : WIDE - HD], HD), (last, WIDE - HD)):
-        part = part.astype(BF16)
-        for t in range(2):
-            send8[:, t * R : t * R + R, start : start + part.shape[1]] = part[t * HD : t * HD + HD].reshape(
-                ND, R, part.shape[1]
-            )
-
-    to_chips(lambda p, q: remote(7, send8.at[q], recv8.at[d], (p, q, m)))
-    recv8[d] = send8[d]
-    arrived(7, recv8.at[pl.ds(0, ND - 1)])
-    logits = jnp.sum(recv8[...].astype(F32), axis=0)
-    lanes = iota((2 * R, WIDE), 1)
+    lanes = iota((ND * R, HD), 1)
+    for t in range(2):
+        sums = uz[t].reshape(ND * R, HD)
+        squares = jnp.sum(sums.astype(F32) * sums.astype(F32), axis=1, keepdims=True)
+        upper = squares.astype(BF16).astype(F32)
+        marks = jnp.where(lax.rem(lanes, 64) < 32, upper, squares - upper)
+        partial = dot(sums, voc_v[...])
+        first = jnp.where((lanes < 64) & (g == 1), marks, partial[:, :HD])
+        last = jnp.where((lanes >= 64) & (g == 0), marks, partial[:, WIDE - HD :])
+        for part, start in ((first, 0), (partial[:, HD : WIDE - HD], HD), (last, WIDE - HD)):
+            width = part.shape[1]
+            send8[t, :, :, start : start + width] = part.astype(BF16).reshape(ND, R, width)
+
+        to_chips(lambda p, q: remote(6 + t, send8.at[t, q], recv8.at[t, d], (p, q, m)))
+    for t in range(2):
+        recv8[t, d] = send8[t, d]
+    lanes = iota((R, WIDE), 1)
     spare = ((lanes < 64) & (g == 1)) | ((lanes >= HALF) & (g == 0))
-    squares = jnp.sum(jnp.where(spare, logits, 0.0), axis=1, keepdims=True) * (1.0 / 32)
-    logits = logits * lax.rsqrt(squares / D + EPSILON)
-    logits = logits[R:] + guidance * (logits[:R] - logits[R:])
+    streams = []
+    for t in range(2):
+        arrived(6 + t, recv8.at[t, pl.ds(0, ND - 1)])
+        logits = jnp.sum(recv8[t].astype(F32), axis=0)
+        squares = jnp.sum(jnp.where(spare, logits, 0.0), axis=1, keepdims=True) * (1.0 / 32)
+        streams.append(logits * lax.rsqrt(squares / D + EPSILON))
+    logits = streams[1] + guidance * (streams[0] - streams[1])
     logits = jnp.where(g == 0, logits, pltpu.roll(logits, WIDE - 64, axis=1))
     for r in range(R):
         out_ref[r] = logits[r : r + 1, :HALF]
@@ -358,7 +359,8 @@
     sent(3, recv4.at[pl.ds(0, NP - 1)])
     sent(4, recv5.at[pl.ds(0, NZ - 1)])
     sent(5, recv5.at[pl.ds(0, NZ - 1)])
-    sent(7, recv8.at[pl.ds(0, ND - 1)])
+    for t in range(2):
+        sent(6 + t, recv8.at[t, pl.ds(0, ND - 1)])
     sent(8, voc_v.at[pl.ds(0, 64), :])
     sent(9, rrecv.at[pl.ds(0, ND - 1)])
 
@@ -403,8 +405,8 @@
             pltpu.VMEM((NC, 16, HD), BF16),
             pltpu.VMEM((NZ, 16, HD), BF16),
             pltpu.VMEM((2, NC, 16, HD), BF16),
-            pltpu.VMEM((ND, 16, WIDE), BF16),
-            pltpu.VMEM((ND, 16, WIDE), BF16),
+            pltpu.VMEM((2, ND, R, WIDE), BF16),
+            pltpu.VMEM((2, ND, R, WIDE), BF16),
             pltpu.SemaphoreType.DMA((16,)),
             pltpu.SemaphoreType.DMA((10,)),
             pltpu.SemaphoreType.DMA((10,)),

time: 59.8 us -> 60 us (level)
  no operation moved by 1% of the time
where the time goes in v6:
time: 60 us; the launch traced here: 59.9 us
  Pallas kernels  59.3 us (99%)
  local copies, waits for them, and re-layouts  0.61 us (1%)
    pallas_call x1, Pallas kernels, body(): pl.pallas_call(kernel, out_shape=pltpu.VMEM((R, 1, HALF), F32), in_specs=...  59.3 us

profile of v6, /device:TPU:1, one launch (start us, length us, event | category | flops | bytes accessed | tf_op | source)
XLA Modules:
  0.0 59.9 jit_solution(11958227356802642243)
XLA Ops:
  0.0 59.3 %shard_map.118 = f32[8,1,832]{2,1,0:T(1,128)S(1)} custom-call(bf16[1,8,2048]{2,1,0:T(8,128)(2,1)} %states_h.1, s32[1,8]{1,0:T(1,128)} %lengths_h.1, bf16[1,8,1,2,4,128]{5,4,3,2,1,0:T(4,128)(2,1)} %sink_h.1, bf16[1,8,1,2,256,128]{5,4,3,2,1,0:T(8,128)(2,1)} %window_h.1, bf16[3,2048,128]{2,1,0:T(8,128)(2,1)} %bitcast.12, bf16[1,128,2048]{2,1,0:T(8,128)(2,1)} %outw_h.1, ...), custom_call_target="tpu_custom_call" | custom-call | tf_op jit(solution)/shard_map/pallas_call | solution.py:375
  59.3 0.6 %copy.16 = f32[8,1,1,832]{3,2,1,0:T(1,128)} copy(f32[8,1,1,832]{3,2,1,0:T(1,128)S(1)} %bitcast.11) | data formatting | bytes 53248
